TPU v7x, 256 devices: a whole 4x4x8 slice. The times are simulated.
256 devices in a mesh: space: 64 (over z, x, core), chan: 4 (over y).
Axes of the slice: x: 4, y: 4, z: 8, core: 2. Of those that a mesh axis runs over, the one named last changes fastest.
Arguments:
- features: float32 [256, 32768], P('chan', 'space'), may hold values from -6 to 6
- positions: float32 [3, 32768], P(None, 'space'), may hold values from 0 to 2, as said below
- counts: int32 [128], P('space'), may hold values from 1 to 256, as said below
- neighbours: int32 [128, 4], P('space'), may hold values from 0 to 5, as said below
- wavevectors: int32 [3, 512], replicated, may hold values from -4 to 4, as said below
- filters: float32 [8, 256, 256], P(None, 'chan'), may hold values from -0.125 to 0.125
- cotangent: float32 [256, 32768], P('chan', 'space'), may hold values from -6 to 6
Outputs:
- updated: float32 [256, 32768], P('chan', 'space')
- grad_features: float32 [256, 32768], P('chan', 'space')
Inputs may be any that keep to these rules, and one draw needn't show every extreme that they name: `counts`: at least one block holds 256 live atoms. `neighbours`: entry e names block e mod 2 of the previous (e // 2 = 0), the same (1) or the next (2) slab layer, the layers closing into a loop; the first entry of a row is the block itself, the entries of a row differ, and each names a block whose position within its layer differs from the row's by at most one. `wavevectors`: no column is all zeros. `positions`: the first coordinate lies in [0, 1], the second in [b, b + 1] for the b-th block of a layer, the third in [0, 1].
All inputs are finite; a program needn't handle non-finite values.
Results may differ from a plain program's by a relative error of at most 0.0003.
Values sent between devices are 32-bit elements; how exact they have to be, the bound alone decides.
No kernel may reach another device: no remote copies, remote signals or barrier semaphores. Data moves between devices by JAX's collectives and lax.ppermute only.
A program may use at most 64 MiB of HBM per device.

v0:
```python
import math

import jax
import jax.numpy as jnp
import numpy as np
from jax import lax
from jax.experimental import pallas as pl
from jax.experimental.pallas import tpu as pltpu
from jax.sharding import PartitionSpec as P

NRAD = 8
CAP = 256
LAYER = 512
HALF = 384
ROWS = 64
PACK = 72
CHUNK = 32
LOG2E = math.log2(math.e)
SCALE = 8.0 * LOG2E
TERM = [0.3 * math.exp(-0.5 * (r - 3.5) ** 2) / SCALE**4 for r in range(NRAD)]
VMEM_BYTES = 56 << 20


vmem = pl.BlockSpec(memory_space=pltpu.VMEM)
smem = pl.BlockSpec(memory_space=pltpu.SMEM)
f32, bf16 = jnp.float32, jnp.bfloat16
NT = (((1,), (1,)), ((), ()))
NN = (((1,), (0,)), ((), ()))


def half_space():
    m = np.arange(HALF)
    nz = (m + 4) % 9 - 4
    rest = (m - nz) // 9
    ny = (rest + 4) % 9 - 4
    nx = (rest - ny) // 9
    return nx, ny, nz


def dot(a, b, dims=NN):
    return lax.dot_general(a, b, dims, preferred_element_type=f32)


def split(value):
    high = value.astype(bf16)
    return high, (value - high.astype(f32)).astype(bf16)


def shape(*dims, dtype=f32):
    return jax.ShapeDtypeStruct(dims, dtype)


def call(kernel, out, n_smem, n_vmem, scratch=()):
    many = isinstance(out, tuple)
    return pl.pallas_call(
        kernel,
        out_shape=out,
        in_specs=[smem] * n_smem + [vmem] * n_vmem,
        out_specs=tuple([vmem] * len(out)) if many else vmem,
        scratch_shapes=list(scratch),
        compiler_params=pltpu.CompilerParams(vmem_limit_bytes=VMEM_BYTES),
    )


def live_row(counts):
    lane = lax.broadcasted_iota(jnp.int32, (1, LAYER), 1)
    bound = jnp.where(lane < CAP, counts[0], counts[1] + CAP)
    return (lane < bound).astype(f32)


def pack_kernel(counts, features, positions, packed):
    live = live_row(counts)
    packed[0:ROWS, :] = features[...] * live
    packed[ROWS : ROWS + 3, :] = positions[...]
    packed[ROWS + 3 : PACK, :] = jnp.broadcast_to(live, (PACK - ROWS - 3, LAYER))


def filter_kernel(filters, forward, backward):
    scaled = jnp.concatenate([filters[r] * TERM[r] for r in range(NRAD)], 0)
    high, low = split(scaled)
    backward[:, 0:256] = high
    backward[:, 256:512] = high
    backward[:, 512:768] = low
    high, low = split(scaled.T)
    forward[:, 0:512] = high
    forward[:, 512:1024] = low
    forward[:, 1024:1536] = high


def trig(turns):
    x = (turns - jnp.round(turns)) * math.pi
    y = x * x
    s = x * (1 + y * (-1 / 6 + y * (1 / 120 + y * (-1 / 5040 + y * (1 / 362880 + y * (-1 / 39916800 + y * (1 / 6227020800)))))))
    c = 1 + y * (-1 / 2 + y * (1 / 24 + y * (-1 / 720 + y * (1 / 40320 + y * (-1 / 3628800 + y * (1 / 479001600))))))
    return 1 - 2 * s * s, 2 * s * c


def structure_kernel(packed, cotangent, digits, keep, send, cot_masked, table_high, table_low, sums):
    space = lax.axis_index("space")
    core, x = space % 2, (space // 2) % 4
    row_x = (packed[ROWS : ROWS + 1, :] + space.astype(f32)) * (1 / 64)
    row_y = packed[ROWS + 1 : ROWS + 2, :] * 0.5
    row_z = packed[ROWS + 2 : ROWS + 3, :]

    def chunk(step, carry):
        first = pl.multiple_of(step * CHUNK, CHUNK)
        rows = pl.ds(first, CHUNK)
        later = pl.ds(first + HALF, CHUNK)
        turns = digits[rows, 0:1] * row_x + digits[rows, 1:2] * row_y + digits[rows, 2:3] * row_z
        cos, sin = trig(turns)
        high, low = split(cos)
        table_high[rows, :] = high
        table_low[rows, :] = low
        high, low = split(sin)
        table_high[later, :] = high
        table_low[later, :] = low
        return carry

    lax.fori_loop(0, HALF // CHUNK, chunk, 0)
    masked_high, masked_low = split(packed[0:ROWS, :])
    cot = cotangent[...] * packed[ROWS + 3 : ROWS + 4, :]
    cot_masked[...] = cot
    cot_high, cot_low = split(cot)
    fields = jnp.concatenate([masked_high, cot_high, masked_low, cot_low], 0)
    both = dot(fields, table_high[...], NT) + dot(fields, table_low[...], NT)
    sums[...] = both[:128] + both[128:]
    for d in range(4):
        rows = slice(16 * d, 16 * d + 16)
        place = 16 * jnp.bitwise_xor(x, d)
        keep[rows, :] = sums[pl.ds(pl.multiple_of(core * ROWS + place, 16), 16), :]
        send[rows, :] = sums[pl.ds(pl.multiple_of((1 - core) * ROWS + place, 16), 16), :]


def radial_terms(col, row):
    dx, dy, dz = (col[a] - row[a] for a in range(3))
    square = jnp.minimum(dx * dx + dy * dy + dz * dz, SCALE * SCALE)
    inside = SCALE * SCALE - square
    u = square * lax.rsqrt(jnp.maximum(square, 1e-20)) - 4.0 * LOG2E
    bend = u * (0.5 / LOG2E)
    base = inside * inside
    up, down = jnp.exp2(u), jnp.exp2(-u)
    terms = [None] * NRAD
    terms[4] = base * jnp.exp2(u * (0.5 - bend))
    terms[3] = base * jnp.exp2(u * (-0.5 - bend))
    for k in range(3):
        terms[5 + k] = terms[4 + k] * up
        terms[2 - k] = terms[3 - k] * down
    return terms


def layer_setup(sources, columns, lines, amounts):
    own = sources[1]
    flipped = own[ROWS:PACK, :].T * SCALE
    for a in range(3):
        columns[a] = jnp.broadcast_to(flipped[:, a : a + 1], (LAYER, 128))
    for section, source in enumerate(sources):
        for side in range(2):
            lanes = slice(side * CAP, (side + 1) * CAP)
            amounts[2 * section + side] = jnp.sum(source[ROWS + 3 : ROWS + 4, lanes]).astype(jnp.int32)
        for side in range(4):
            for a in range(3):
                at = slice(ROWS + a, ROWS + a + 1)
                shift = (section - 1.0) * SCALE if a == 0 else 0.0
                lines[4 * section + side, a : a + 1, :] = source[at, 128 * side : 128 * side + 128] * SCALE + shift


def visit(neighbours, amounts, columns, lines, flush, store):
    def outer(index, carry):
        block, entry, side = index // 8, (index // 2) % 4, index % 2
        chosen = neighbours[block, entry]
        piece = 2 * chosen + side
        trips = jnp.where(side * 128 < amounts[chosen], (amounts[2 + block] + 127) // 128, 0)

        def inner(step, last):
            flush(*last)
            where = 2 * block + step
            at = pl.ds(pl.multiple_of(where * 128, 128), 128)
            col = [columns[a, at, :] for a in range(3)]
            row = [lines[piece, a : a + 1, :] for a in range(3)]
            store(radial_terms(col, row))
            return where, piece

        return lax.fori_loop(0, trips, inner, carry)

    flush(*lax.fori_loop(0, 16, outer, (jnp.int32(0), jnp.int32(0))))


def forward_kernel(neighbours, own, below, above, filters, own_panel, third_panel, near_panel, far_panel,
                   columns, lines, amounts, values, highs, lows, sums, share):
    mine = lax.axis_index("chan")
    layer_setup((below, own, above), columns, lines, amounts)
    for section, source in enumerate((below, own, above)):
        high, low = split(source[0:ROWS, :])
        for side in range(4):
            values[4 * section + side, 0:ROWS, :] = high[:, 128 * side : 128 * side + 128]
            values[4 * section + side, ROWS:128, :] = low[:, 128 * side : 128 * side + 128]
    sums[...] = jnp.zeros_like(sums)
    highs[...] = jnp.zeros_like(highs)
    lows[...] = jnp.zeros_like(lows)

    def flush(where, piece):
        value = values[piece]
        out = dot(
            jnp.concatenate([highs[...], lows[...]], 1), jnp.concatenate([value, value], 1), NT
        )
        rows = pl.ds(pl.multiple_of(where * 1024, 1024), 1024)
        sums[rows, :] = sums[rows, :] + out

    def store(terms):
        for r, term in enumerate(terms):
            high, low = split(term)
            highs[128 * r : 128 * r + 128, :] = high
            lows[128 * r : 128 * r + 128, :] = low

    visit(neighbours, amounts, columns, lines, flush, store)
    lane = lax.broadcasted_iota(jnp.int32, (128, 128), 1)
    for where in range(4):
        pieces = []
        for r in range(0, NRAD, 2):
            even = sums[where * 1024 + 128 * r : where * 1024 + 128 * r + 128, :]
            odd = sums[where * 1024 + 128 * r + 128 : where * 1024 + 128 * r + 256, :]
            pieces.append(
                jnp.where(lane < ROWS, even, odd)
                + jnp.where(lane < ROWS, pltpu.roll(even, ROWS, 1), pltpu.roll(odd, ROWS, 1))
            )
        first, second = zip(*[split(p) for p in pieces])
        right = jnp.concatenate([*first, *first, *second], 1)
        share[:, 128 * where : 128 * where + 128] = dot(filters[...], right, NT)
    for out, flip in ((own_panel, 0), (third_panel, 3), (near_panel, 1), (far_panel, 2)):
        out[...] = share[pl.ds(pl.multiple_of(ROWS * jnp.bitwise_xor(mine, flip), ROWS), ROWS), :]


def activation_kernel(own_panel, near, third, cot_masked, activated, upstream):
    pre = own_panel[...] + near[...] + third[...]
    sigma = 1.0 / (1.0 + jnp.exp(-pre))
    activated[...] = pre * sigma
    upstream[...] = cot_masked[...] * (sigma * (1.0 + pre * (1.0 - sigma)))


def backward_kernel(neighbours, own, below, above, filters, mine_up, third_up, near_up, far_up,
                    left, middle, right, columns, lines, amounts, panels, cots, tiles, sums):
    mine = lax.axis_index("chan")
    layer_setup((below, own, above), columns, lines, amounts)
    ups = [mine_up[...], third_up[...], near_up[...], far_up[...]]
    for value, flip in zip(ups, (0, 3, 1, 2)):
        first, second = split(value)
        at = ROWS * jnp.bitwise_xor(mine, flip)
        panels[pl.ds(pl.multiple_of(at, ROWS), ROWS), :] = first
        panels[pl.ds(pl.multiple_of(at + 256, ROWS), ROWS), :] = second
        panels[pl.ds(pl.multiple_of(at + 512, ROWS), ROWS), :] = first
    cot = dot(filters[...], panels[...])
    for r in range(NRAD):
        first, second = split(cot[ROWS * r : ROWS * r + ROWS])
        for where in range(4):
            cots[NRAD * where + r, 0:ROWS, :] = first[:, 128 * where : 128 * where + 128]
            cots[NRAD * where + r, ROWS:128, :] = second[:, 128 * where : 128 * where + 128]
    sums[...] = jnp.zeros_like(sums)
    tiles[...] = jnp.zeros_like(tiles)

    def flush(where, piece):
        parts = []
        for r in range(NRAD):
            parts += [cots[NRAD * where + r]] * 2
        rows = pl.ds(pl.multiple_of(piece * 128, 128), 128)
        sums[rows, :] = sums[rows, :] + dot(jnp.concatenate(parts, 1), tiles[...])

    def store(terms):
        for r, term in enumerate(terms):
            high, low = split(term)
            tiles[256 * r : 256 * r + 128, :] = high
            tiles[256 * r + 128 : 256 * r + 256, :] = low

    visit(neighbours, amounts, columns, lines, flush, store)
    for section, out in enumerate((left, middle, right)):
        for side in range(4):
            at = 128 * (4 * section + side)
            out[:, 128 * side : 128 * side + 128] = sums[at : at + ROWS, :] + sums[at + ROWS : at + 128, :]


def project_kernel(mine_half, other_half, weights, table_high, table_low, packed, activated, cot_masked, middle,
                   updated, partial, scratch):
    space = lax.axis_index("space")
    core, x = space % 2, (space // 2) % 4
    for half, at in ((mine_half, core), (other_half, 1 - core)):
        scaled = half[...] * weights[...]
        for d in range(4):
            place = at * ROWS + 16 * jnp.bitwise_xor(x, d)
            first, second = split(scaled[16 * d : 16 * d + 16])
            scratch[pl.ds(pl.multiple_of(place, 16), 16), :] = first
            scratch[pl.ds(pl.multiple_of(place + 128, 16), 16), :] = second
    both = dot(scratch[...], table_high[...]) + dot(scratch[...], table_low[...])
    live = packed[ROWS + 3 : ROWS + 4, :]
    updated[...] = live * (packed[0:ROWS, :] + activated[...] + (both[:ROWS] + both[128 : 128 + ROWS]))
    partial[...] = live * (cot_masked[...] + middle[...] + (both[ROWS:128] + both[128 + ROWS :]))


def wave_weights(wavevectors, n_space, slots):
    code = jnp.abs(81 * wavevectors[0] + 9 * wavevectors[1] + wavevectors[2])
    copies = jnp.sum((code[:, None] == jnp.arange(HALF)[None, :]).astype(f32), 0)
    nx, ny, nz = half_space()
    qx, qy, qz = 2 * math.pi / 64 * nx, math.pi * ny, 2 * math.pi * nz
    square = qx * qx + qy * qy + qz * qz
    screened = jnp.asarray(np.exp(-square / 2000.0) / (square + 100.0), f32)
    factor = math.sqrt(3.0 / (n_space * slots))
    weights = factor * copies * screened / jnp.sqrt(jnp.sum(copies * screened * screened))
    return jnp.concatenate([weights, weights])[None]


def shards(features, positions, counts, neighbours, wavevectors, filters, cotangent):
    n_space = lax.axis_size("space")

    def shift(v, d):
        return lax.ppermute(v, "space", [(i, (i + d) % n_space) for i in range(n_space)])

    def swap(v, mask):
        return lax.ppermute(v, "space", [(i, i ^ mask) for i in range(n_space)])

    def chan_swap(v, mask):
        return lax.ppermute(v, "chan", [(i, i ^ mask) for i in range(4)])

    packed = call(pack_kernel, shape(PACK, LAYER), 1, 2)(counts, features, positions)
    below = shift(packed, 1)
    above = shift(packed, -1)

    digits = np.zeros((HALF, 8), np.float32)
    digits[:, :3] = np.stack(half_space(), 1)
    keep, send, cot_masked, table_high, table_low = call(
        structure_kernel,
        (shape(ROWS, 768), shape(ROWS, 768), shape(ROWS, LAYER),
         shape(768, LAYER, dtype=bf16), shape(768, LAYER, dtype=bf16)),
        0, 3, [pltpu.VMEM((128, 768), f32)],
    )(packed, cotangent, jnp.asarray(digits))
    forward_filters, backward_filters = call(
        filter_kernel, (shape(256, 1536, dtype=bf16), shape(512, 768, dtype=bf16)), 0, 1
    )(filters)
    weights = wave_weights(wavevectors, n_space, LAYER)

    half = keep + swap(send, 1)
    got = []
    for d in (1, 2, 3):
        got.append(swap(half[16 * d : 16 * d + 16], 2 * d))

    own_panel, third_panel, near_panel, far_panel = call(
        forward_kernel, tuple([shape(ROWS, LAYER)] * 4), 1, 4,
        [
            pltpu.VMEM((3, LAYER, 128), f32),
            pltpu.VMEM((12, 8, 128), f32),
            pltpu.SMEM((6,), jnp.int32),
            pltpu.VMEM((12, 128, 128), bf16),
            pltpu.VMEM((1024, 128), bf16),
            pltpu.VMEM((1024, 128), bf16),
            pltpu.VMEM((4096, 128), f32),
            pltpu.VMEM((256, LAYER), f32),
        ],
    )(neighbours, packed, below, above, forward_filters)
    quarter = half[:16] + got[0] + got[1] + got[2]
    far = chan_swap(far_panel, 1)
    near = chan_swap(near_panel, 1)
    quarter = quarter + swap(quarter, 32)
    third_panel = third_panel + far
    third = chan_swap(third_panel, 3)
    quarter = quarter + swap(quarter, 16)
    activated, upstream = call(
        activation_kernel, (shape(ROWS, LAYER), shape(ROWS, LAYER)), 0, 4
    )(own_panel, near, third, cot_masked)
    third_up = chan_swap(upstream, 3)
    near_up = chan_swap(upstream, 1)
    quarter = quarter + swap(quarter, 8)
    far_up = chan_swap(third_up, 1)
    got = []
    for d in (1, 2, 3):
        got.append(swap(quarter, 2 * d))
    left, middle, right = call(
        backward_kernel, tuple([shape(ROWS, LAYER)] * 3), 1, 8,
        [
            pltpu.VMEM((3, LAYER, 128), f32),
            pltpu.VMEM((12, 8, 128), f32),
            pltpu.SMEM((6,), jnp.int32),
            pltpu.VMEM((768, LAYER), bf16),
            pltpu.VMEM((32, 128, 128), bf16),
            pltpu.VMEM((2048, 128), bf16),
            pltpu.VMEM((1536, 128), f32),
        ],
    )(neighbours, packed, below, above, backward_filters, upstream, third_up, near_up, far_up)
    half = jnp.concatenate([quarter, *got], 0)
    from_lower = shift(right, 1)
    from_upper = shift(left, -1)
    other = swap(half, 1)
    updated, partial = call(
        project_kernel, (shape(ROWS, LAYER), shape(ROWS, LAYER)), 0, 9,
        [pltpu.VMEM((256, 768), bf16)],
    )(half, other, weights, table_high, table_low, packed, activated, cot_masked, middle)
    grad_features = partial + packed[ROWS + 3][None] * (from_lower + from_upper)
    return updated, grad_features


def solution(mesh):
    return jax.shard_map(
        shards,
        mesh=mesh,
        in_specs=(
            P("chan", "space"),
            P(None, "space"),
            P("space"),
            P("space", None),
            P(),
            P(None, "chan", None),
            P("chan", "space"),
        ),
        out_specs=(P("chan", "space"), P("chan", "space")),
        check_vma=False,
    )
```

profile of v0, /device:TPU:111, one launch (start us, length us, event | category | flops | bytes accessed | tf_op | source)
XLA Modules:
  0.0 85.5 jit_solution(12732708596416592491)
XLA Ops:
  0.6 1.6 %shard_map.104.packed.own = f32[72,512]{1,0:T(8,128)} custom-call(s32[2]{0:T(128)} %counts.1, f32[64,512]{1,0:T(8,128)} %features.1, f32[3,512]{1,0:T(4,128)} %positions.1), custom_call_target="tpu_custom_call" | custom-call | tf_op jit(solution)/shard_map/pallas_call | solution.py:321
  2.2 4.5 %shard_map.105 = (f32[64,768]{1,0:T(8,128)}, f32[64,768]{1,0:T(8,128)}, f32[64,512]{1,0:T(8,128)}, bf16[768,512]{1,0:T(8,128)(2,1)}, bf16[768,512]{1,0:T(8,128)(2,1)}) custom-call(f32[72,512]{1,0:T(8,128)} %shard_map.104.packed.own, f32[64,512]{1,0:T(8,128)} %cotangent.1, f32[384,8]{1,0:T(8,128)} %constant.12.clone.digits), custom_call_target="tpu_custom_call" | custom-call | tf_op jit(solution)/shard_map/pallas_call | solution.py:327
  7.4 2.7 %collective-permute-start.11 = (f32[72,512]{1,0:T(8,128)S(1)}, f32[72,512]{1,0:T(8,128)S(1)}, u32[]{:S(2)}, u32[]{:S(2)}) collective-permute-start(f32[72,512]{1,0:T(8,128)S(1)} %copy-done), channel_id=1, source_target_pairs={{0,4},{4,8},{8,12},{12,16},{16,20},{20,24},{24,28},{28,32},{32,36}... | collective-permute-start | bytes 442376 | tf_op jit(solution)/shard_map/ppermute | solution.py:313
  10.2 2.3 %shard_map.106 = (bf16[256,1536]{1,0:T(8,128)(2,1)}, bf16[512,768]{1,0:T(8,128)(2,1)}) custom-call(f32[8,64,256]{2,1,0:T(8,128)} %filters.1), custom_call_target="tpu_custom_call" | custom-call | tf_op jit(solution)/shard_map/pallas_call | solution.py:333
  12.5 5.6 %collective-permute-done.12.above = f32[72,512]{1,0:T(8,128)S(1)} collective-permute-done((f32[72,512]{1,0:T(8,128)S(1)}, f32[72,512]{1,0:T(8,128)S(1)}, u32[]{:S(2)}, u32[]{:S(2)}) %collective-permute-start.12) | collective-permute-done | bytes 147488 | tf_op jit(solution)/shard_map/ppermute | solution.py:313
  18.7 7.6 %shard_map.107 = (f32[64,512]{1,0:T(8,128)}, f32[64,512]{1,0:T(8,128)}, f32[64,512]{1,0:T(8,128)}, f32[64,512]{1,0:T(8,128)}) custom-call(s32[2,4]{1,0:T(2,128)} %neighbours.3, f32[72,512]{1,0:T(8,128)} %shard_map.104.packed.own, f32[72,512]{1,0:T(8,128)} %copy-done.2, f32[72,512]{1,0:T(8,128)} %copy-done.3, bf16[256,1536]{1,0:T(8,128)(2,1)} %get-tuple-element.24.filters), custom_call_target="tpu_custom_call" | custom-call | tf_op jit(solution)/shard_map/pallas_call | solution.py:343
  26.7 1.0 %collective-permute-start.2 = (f32[16,768]{1,0:T(8,128)S(1)}, f32[16,768]{1,0:T(8,128)S(1)}, u32[]{:S(2)}, u32[]{:S(2)}) collective-permute-start(f32[16,768]{1,0:T(8,128)S(1)} %get-tuple-element.40), channel_id=1, source_target_pairs={{0,16},{4,20},{8,24},{12,28},{16,0},{20,4},{24,8},{28,12},{32,48},... | collective-permute-start | bytes 147464 | tf_op jit(solution)/shard_map/ppermute | solution.py:316
  27.6 2.9 %collective-permute-start.3 = (f32[16,768]{1,0:T(8,128)S(1)}, f32[16,768]{1,0:T(8,128)S(1)}, u32[]{:S(2)}, u32[]{:S(2)}) collective-permute-start(f32[16,768]{1,0:T(8,128)S(1)} %get-tuple-element.39), channel_id=1, source_target_pairs={{0,24},{4,28},{8,16},{12,20},{16,8},{20,12},{24,0},{28,4},{32,56},... | collective-permute-start | bytes 147464 | tf_op jit(solution)/shard_map/ppermute | solution.py:316
  30.5 1.3 %collective-permute-start.13 = (f32[64,512]{1,0:T(8,128)S(1)}, f32[64,512]{1,0:T(8,128)S(1)}, u32[]{:S(2)}, u32[]{:S(2)}) collective-permute-start(f32[64,512]{1,0:T(8,128)S(1)} %copy-done.16), channel_id=1, source_target_pairs={{0,1},{1,0},{2,3},{3,2},{4,5},{5,4},{6,7},{7,6},{8,9},{9,8},{10,11... | collective-permute-start | bytes 393224 | tf_op jit(solution)/shard_map/ppermute | solution.py:319
  31.8 1.4 %collective-permute-start.15 = (f32[64,512]{1,0:T(8,128)S(1)}, f32[64,512]{1,0:T(8,128)S(1)}, u32[]{:S(2)}, u32[]{:S(2)}) collective-permute-start(f32[64,512]{1,0:T(8,128)S(1)} %add.55), channel_id=1, source_target_pairs={{0,3},{1,2},{2,1},{3,0},{4,7},{5,6},{6,5},{7,4},{8,11},{9,10},{10,... | collective-permute-start | bytes 393224 | tf_op jit(solution)/shard_map/ppermute | solution.py:319
  33.3 3.1 %collective-permute-start.4 = (f32[16,768]{1,0:T(8,128)S(1)}, f32[16,768]{1,0:T(8,128)S(1)}, u32[]{:S(2)}, u32[]{:S(2)}) collective-permute-start(f32[16,768]{1,0:T(8,128)S(1)} %fusion.1), channel_id=1, source_target_pairs={{0,128},{4,132},{8,136},{12,140},{16,144},{20,148},{24,152},{28,15... | collective-permute-start | bytes 147464 | tf_op jit(solution)/shard_map/ppermute | solution.py:316
  36.4 4.2 %collective-permute-done.4 = f32[16,768]{1,0:T(8,128)S(1)} collective-permute-done((f32[16,768]{1,0:T(8,128)S(1)}, f32[16,768]{1,0:T(8,128)S(1)}, u32[]{:S(2)}, u32[]{:S(2)}) %collective-permute-start.4) | collective-permute-done | bytes 49184 | tf_op jit(solution)/shard_map/ppermute | solution.py:316
  41.4 1.9 %shard_map.108 = (f32[64,512]{1,0:T(8,128)}, f32[64,512]{1,0:T(8,128)}) custom-call(f32[64,512]{1,0:T(8,128)} %get-tuple-element.25.own_panel, f32[64,512]{1,0:T(8,128)} %copy-done.11, f32[64,512]{1,0:T(8,128)} %copy-done.12, f32[64,512]{1,0:T(8,128)} %get-tuple-element.29.cot_masked), custom_call_target="tpu_custom_call" | custom-call | tf_op jit(solution)/shard_map/pallas_call | solution.py:363
  43.3 1.2 %collective-permute-start.16 = (f32[64,512]{1,0:T(8,128)}, f32[64,512]{1,0:T(8,128)S(1)}, u32[]{:S(2)}, u32[]{:S(2)}) collective-permute-start(f32[64,512]{1,0:T(8,128)} %get-tuple-element.32.mine_up), channel_id=1, source_target_pairs={{0,3},{1,2},{2,1},{3,0},{4,7},{5,6},{6,5},{7,4},{8,11},{9,10},{10,... | collective-permute-start | bytes 393224 | tf_op jit(solution)/shard_map/ppermute | solution.py:319
  44.7 0.9 %collective-permute-start.6 = (f32[16,768]{1,0:T(8,128)S(1)}, f32[16,768]{1,0:T(8,128)S(1)}, u32[]{:S(2)}, u32[]{:S(2)}) collective-permute-start(f32[16,768]{1,0:T(8,128)S(1)} %add.51), channel_id=1, source_target_pairs={{0,32},{4,36},{8,40},{12,44},{16,48},{20,52},{24,56},{28,60},{32,0... | collective-permute-start | bytes 147464 | tf_op jit(solution)/shard_map/ppermute | solution.py:316
  45.8 2.2 %collective-permute-done.6 = f32[16,768]{1,0:T(8,128)S(1)} collective-permute-done((f32[16,768]{1,0:T(8,128)S(1)}, f32[16,768]{1,0:T(8,128)S(1)}, u32[]{:S(2)}, u32[]{:S(2)}) %collective-permute-start.6) | collective-permute-done | bytes 49184 | tf_op jit(solution)/shard_map/ppermute | solution.py:316
  48.4 3.5 %collective-permute-start.8 = (f32[16,768]{1,0:T(8,128)S(1)}, f32[16,768]{1,0:T(8,128)S(1)}, u32[]{:S(2)}, u32[]{:S(2)}) collective-permute-start(f32[16,768]{1,0:T(8,128)S(1)} %add.52), channel_id=1, source_target_pairs={{0,16},{4,20},{8,24},{12,28},{16,0},{20,4},{24,8},{28,12},{32,48},... | collective-permute-start | bytes 147464 | tf_op jit(solution)/shard_map/ppermute | solution.py:316
  51.9 2.7 %collective-permute-start.17 = (f32[64,512]{1,0:T(8,128)S(1)}, f32[64,512]{1,0:T(8,128)S(1)}, u32[]{:S(2)}, u32[]{:S(2)}) collective-permute-start(f32[64,512]{1,0:T(8,128)S(1)} %copy-done.6), channel_id=1, source_target_pairs={{0,1},{1,0},{2,3},{3,2},{4,5},{5,4},{6,7},{7,6},{8,9},{9,8},{10,11... | collective-permute-start | bytes 393224 | tf_op jit(solution)/shard_map/ppermute | solution.py:319
  56.4 3.0 %collective-permute-start.10 = (f32[64,768]{1,0:T(8,128)S(1)}, f32[64,768]{1,0:T(8,128)S(1)}, u32[]{:S(2)}, u32[]{:S(2)}) collective-permute-start(f32[64,768]{1,0:T(8,128)S(1)} %pad_maximum_fusion.mine_half), channel_id=1, source_target_pairs={{0,4},{4,0},{8,12},{12,8},{16,20},{20,16},{24,28},{28,24},{32,36},... | collective-permute-start | bytes 589832 | tf_op jit(solution)/shard_map/ppermute | solution.py:316
  60.0 6.6 %shard_map.109 = (f32[64,512]{1,0:T(8,128)}, f32[64,512]{1,0:T(8,128)}, f32[64,512]{1,0:T(8,128)}) custom-call(s32[2,4]{1,0:T(2,128)} %neighbours.3, f32[72,512]{1,0:T(8,128)} %shard_map.104.packed.own, f32[72,512]{1,0:T(8,128)} %copy-done.2, f32[72,512]{1,0:T(8,128)} %copy-done.3, bf16[512,768]{1,0:T(8,128)(2,1)} %get-tuple-element.31.filters, ...), custom_call_target="tpu_custom_call" | custom-call | tf_op jit(solution)/shard_map/pallas_call | solution.py:373
  66.6 9.3 %collective-permute-start.19 = (f32[64,512]{1,0:T(8,128)}, f32[64,512]{1,0:T(8,128)S(1)}, u32[]{:S(2)}, u32[]{:S(2)}) collective-permute-start(f32[64,512]{1,0:T(8,128)} %get-tuple-element.36), channel_id=1, source_target_pairs={{0,4},{4,8},{8,12},{12,16},{16,20},{20,24},{24,28},{28,32},{32,36}... | collective-permute-start | bytes 393224 | tf_op jit(solution)/shard_map/ppermute | solution.py:313
  78.0 3.0 %shard_map.110 = (f32[64,512]{1,0:T(8,128)}, f32[64,512]{1,0:T(8,128)}) custom-call(f32[64,768]{1,0:T(8,128)} %copy-done.1, f32[64,768]{1,0:T(8,128)} %copy-done.5, f32[1,768]{1,0:T(1,128)} %broadcast_in_dim.2.weights, bf16[768,512]{1,0:T(8,128)(2,1)} %get-tuple-element.22.table_high, bf16[768,512]{1,0:T(8,128)(2,1)} %get-tuple-element.23.table_low, ...), custom_call_target="tpu_custom_call" | custom-call | tf_op jit(solution)/shard_map/pallas_call | solution.py:389
  81.0 2.9 %collective-permute-done.20 = f32[64,512]{1,0:T(8,128)S(1)} collective-permute-done((f32[64,512]{1,0:T(8,128)}, f32[64,512]{1,0:T(8,128)S(1)}, u32[]{:S(2)}, u32[]{:S(2)}) %collective-permute-start.20) | collective-permute-done | bytes 131104 | tf_op jit(solution)/shard_map/ppermute | solution.py:313
  83.9 1.6 %multiply_add_fusion = f32[64,512]{1,0:T(8,128)} fusion(f32[64,512]{1,0:T(8,128)} %get-tuple-element.35, f32[64,512]{1,0:T(8,128)S(1)} %collective-permute-done.19, f32[64,512]{1,0:T(8,128)S(1)} %collective-permute-done.20, f32[512]{0:T(512)S(1)} %bitcast.2), kind=kLoop, calls=%fused_computation.3 | loop fusion | flops 98304 | bytes 526336 | tf_op jit(solution)/shard_map/add | solution.py:393
  (75 shorter events, 7.1 us)
Async XLA Ops:
  6.8 19.7 %collective-permute-start = (f32[64,768]{1,0:T(8,128)}, f32[64,768]{1,0:T(8,128)S(1)}, u32[]{:S(2)}, u32[]{:S(2)}) collective-permute-start(f32[64,768]{1,0:T(8,128)} %get-tuple-element.21), channel_id=1, source_target_pairs={{0,4},{4,0},{8,12},{12,8},{16,20},{20,16},{24,28},{28,24},{32,36},... | collective-permute-start | bytes 589832 | tf_op jit(solution)/shard_map/ppermute | solution.py:316
  7.4 5.0 %collective-permute-start.11 = (f32[72,512]{1,0:T(8,128)S(1)}, f32[72,512]{1,0:T(8,128)S(1)}, u32[]{:S(2)}, u32[]{:S(2)}) collective-permute-start(f32[72,512]{1,0:T(8,128)S(1)} %copy-done), channel_id=1, source_target_pairs={{0,4},{4,8},{8,12},{12,16},{16,20},{20,24},{24,28},{28,32},{32,36}... | collective-permute-start | bytes 442376 | tf_op jit(solution)/shard_map/ppermute | solution.py:313
  10.2 7.9 %collective-permute-start.12 = (f32[72,512]{1,0:T(8,128)S(1)}, f32[72,512]{1,0:T(8,128)S(1)}, u32[]{:S(2)}, u32[]{:S(2)}) collective-permute-start(f32[72,512]{1,0:T(8,128)S(1)} %copy-done), channel_id=1, source_target_pairs={{0,252},{4,0},{8,4},{12,8},{16,12},{20,16},{24,20},{28,24},{32,28}... | collective-permute-start | bytes 442376 | tf_op jit(solution)/shard_map/ppermute | solution.py:313
  26.3 5.5 %collective-permute-start.14 = (f32[64,512]{1,0:T(8,128)}, f32[64,512]{1,0:T(8,128)S(1)}, u32[]{:S(2)}, u32[]{:S(2)}) collective-permute-start(f32[64,512]{1,0:T(8,128)} %get-tuple-element.28), channel_id=1, source_target_pairs={{0,1},{1,0},{2,3},{3,2},{4,5},{5,4},{6,7},{7,6},{8,9},{9,8},{10,11... | collective-permute-start | bytes 393224 | tf_op jit(solution)/shard_map/ppermute | solution.py:319
  26.6 6.7 %collective-permute-start.1 = (f32[16,768]{1,0:T(8,128)S(1)}, f32[16,768]{1,0:T(8,128)S(1)}, u32[]{:S(2)}, u32[]{:S(2)}) collective-permute-start(f32[16,768]{1,0:T(8,128)S(1)} %get-tuple-element.38), channel_id=1, source_target_pairs={{0,8},{4,12},{8,0},{12,4},{16,24},{20,28},{24,16},{28,20},{32,40},... | collective-permute-start | bytes 147464 | tf_op jit(solution)/shard_map/ppermute | solution.py:316
  26.7 6.6 %collective-permute-start.2 = (f32[16,768]{1,0:T(8,128)S(1)}, f32[16,768]{1,0:T(8,128)S(1)}, u32[]{:S(2)}, u32[]{:S(2)}) collective-permute-start(f32[16,768]{1,0:T(8,128)S(1)} %get-tuple-element.40), channel_id=1, source_target_pairs={{0,16},{4,20},{8,24},{12,28},{16,0},{20,4},{24,8},{28,12},{32,48},... | collective-permute-start | bytes 147464 | tf_op jit(solution)/shard_map/ppermute | solution.py:316
  27.6 5.6 %collective-permute-start.3 = (f32[16,768]{1,0:T(8,128)S(1)}, f32[16,768]{1,0:T(8,128)S(1)}, u32[]{:S(2)}, u32[]{:S(2)}) collective-permute-start(f32[16,768]{1,0:T(8,128)S(1)} %get-tuple-element.39), channel_id=1, source_target_pairs={{0,24},{4,28},{8,16},{12,20},{16,8},{20,12},{24,0},{28,4},{32,56},... | collective-permute-start | bytes 147464 | tf_op jit(solution)/shard_map/ppermute | solution.py:316
  30.5 10.2 %collective-permute-start.13 = (f32[64,512]{1,0:T(8,128)S(1)}, f32[64,512]{1,0:T(8,128)S(1)}, u32[]{:S(2)}, u32[]{:S(2)}) collective-permute-start(f32[64,512]{1,0:T(8,128)S(1)} %copy-done.16), channel_id=1, source_target_pairs={{0,1},{1,0},{2,3},{3,2},{4,5},{5,4},{6,7},{7,6},{8,9},{9,8},{10,11... | collective-permute-start | bytes 393224 | tf_op jit(solution)/shard_map/ppermute | solution.py:319
  31.8 8.9 %collective-permute-start.15 = (f32[64,512]{1,0:T(8,128)S(1)}, f32[64,512]{1,0:T(8,128)S(1)}, u32[]{:S(2)}, u32[]{:S(2)}) collective-permute-start(f32[64,512]{1,0:T(8,128)S(1)} %add.55), channel_id=1, source_target_pairs={{0,3},{1,2},{2,1},{3,0},{4,7},{5,6},{6,5},{7,4},{8,11},{9,10},{10,... | collective-permute-start | bytes 393224 | tf_op jit(solution)/shard_map/ppermute | solution.py:319
  33.3 7.3 %collective-permute-start.4 = (f32[16,768]{1,0:T(8,128)S(1)}, f32[16,768]{1,0:T(8,128)S(1)}, u32[]{:S(2)}, u32[]{:S(2)}) collective-permute-start(f32[16,768]{1,0:T(8,128)S(1)} %fusion.1), channel_id=1, source_target_pairs={{0,128},{4,132},{8,136},{12,140},{16,144},{20,148},{24,152},{28,15... | collective-permute-start | bytes 147464 | tf_op jit(solution)/shard_map/ppermute | solution.py:316
  40.6 4.0 %collective-permute-start.5 = (f32[16,768]{1,0:T(8,128)S(1)}, f32[16,768]{1,0:T(8,128)S(1)}, u32[]{:S(2)}, u32[]{:S(2)}) collective-permute-start(f32[16,768]{1,0:T(8,128)S(1)} %add.50), channel_id=1, source_target_pairs={{0,64},{4,68},{8,72},{12,76},{16,80},{20,84},{24,88},{28,92},{32,9... | collective-permute-start | bytes 147464 | tf_op jit(solution)/shard_map/ppermute | solution.py:316
  43.3 11.4 %collective-permute-start.16 = (f32[64,512]{1,0:T(8,128)}, f32[64,512]{1,0:T(8,128)S(1)}, u32[]{:S(2)}, u32[]{:S(2)}) collective-permute-start(f32[64,512]{1,0:T(8,128)} %get-tuple-element.32.mine_up), channel_id=1, source_target_pairs={{0,3},{1,2},{2,1},{3,0},{4,7},{5,6},{6,5},{7,4},{8,11},{9,10},{10,... | collective-permute-start | bytes 393224 | tf_op jit(solution)/shard_map/ppermute | solution.py:319
  44.7 3.3 %collective-permute-start.6 = (f32[16,768]{1,0:T(8,128)S(1)}, f32[16,768]{1,0:T(8,128)S(1)}, u32[]{:S(2)}, u32[]{:S(2)}) collective-permute-start(f32[16,768]{1,0:T(8,128)S(1)} %add.51), channel_id=1, source_target_pairs={{0,32},{4,36},{8,40},{12,44},{16,48},{20,52},{24,56},{28,60},{32,0... | collective-permute-start | bytes 147464 | tf_op jit(solution)/shard_map/ppermute | solution.py:316
  45.8 9.0 %copy-start.15 = (f32[384]{0:T(512)S(1)}, f32[384]{0:T(512)}, u32[]{:S(2)}) copy-start(f32[384]{0:T(512)} %constant.16) | copy-start | bytes 4612
  48.0 8.1 %collective-permute-start.7 = (f32[16,768]{1,0:T(8,128)S(1)}, f32[16,768]{1,0:T(8,128)S(1)}, u32[]{:S(2)}, u32[]{:S(2)}) collective-permute-start(f32[16,768]{1,0:T(8,128)S(1)} %add.52), channel_id=1, source_target_pairs={{0,8},{4,12},{8,0},{12,4},{16,24},{20,28},{24,16},{28,20},{32,40},... | collective-permute-start | bytes 147464 | tf_op jit(solution)/shard_map/ppermute | solution.py:316
  48.4 7.7 %collective-permute-start.8 = (f32[16,768]{1,0:T(8,128)S(1)}, f32[16,768]{1,0:T(8,128)S(1)}, u32[]{:S(2)}, u32[]{:S(2)}) collective-permute-start(f32[16,768]{1,0:T(8,128)S(1)} %add.52), channel_id=1, source_target_pairs={{0,16},{4,20},{8,24},{12,28},{16,0},{20,4},{24,8},{28,12},{32,48},... | collective-permute-start | bytes 147464 | tf_op jit(solution)/shard_map/ppermute | solution.py:316
  51.9 4.4 %collective-permute-start.9 = (f32[16,768]{1,0:T(8,128)S(1)}, f32[16,768]{1,0:T(8,128)S(1)}, u32[]{:S(2)}, u32[]{:S(2)}) collective-permute-start(f32[16,768]{1,0:T(8,128)S(1)} %add.52), channel_id=1, source_target_pairs={{0,24},{4,28},{8,16},{12,20},{16,8},{20,12},{24,0},{28,4},{32,56},... | collective-permute-start | bytes 147464 | tf_op jit(solution)/shard_map/ppermute | solution.py:316
  51.9 7.4 %collective-permute-start.17 = (f32[64,512]{1,0:T(8,128)S(1)}, f32[64,512]{1,0:T(8,128)S(1)}, u32[]{:S(2)}, u32[]{:S(2)}) collective-permute-start(f32[64,512]{1,0:T(8,128)S(1)} %copy-done.6), channel_id=1, source_target_pairs={{0,1},{1,0},{2,3},{3,2},{4,5},{5,4},{6,7},{7,6},{8,9},{9,8},{10,11... | collective-permute-start | bytes 393224 | tf_op jit(solution)/shard_map/ppermute | solution.py:319
  54.6 4.7 %collective-permute-start.18 = (f32[64,512]{1,0:T(8,128)S(1)}, f32[64,512]{1,0:T(8,128)S(1)}, u32[]{:S(2)}, u32[]{:S(2)}) collective-permute-start(f32[64,512]{1,0:T(8,128)S(1)} %collective-permute-done.16.third_up), channel_id=1, source_target_pairs={{0,1},{1,0},{2,3},{3,2},{4,5},{5,4},{6,7},{7,6},{8,9},{9,8},{10,11... | collective-permute-start | bytes 393224 | tf_op jit(solution)/shard_map/ppermute | solution.py:319
  56.4 10.3 %copy-start.1 = (f32[64,768]{1,0:T(8,128)}, f32[64,768]{1,0:T(8,128)S(1)}, u32[]{:S(2)}) copy-start(f32[64,768]{1,0:T(8,128)S(1)} %pad_maximum_fusion.mine_half) | copy-start | bytes 589828
  56.4 21.0 %collective-permute-start.10 = (f32[64,768]{1,0:T(8,128)S(1)}, f32[64,768]{1,0:T(8,128)S(1)}, u32[]{:S(2)}, u32[]{:S(2)}) collective-permute-start(f32[64,768]{1,0:T(8,128)S(1)} %pad_maximum_fusion.mine_half), channel_id=1, source_target_pairs={{0,4},{4,0},{8,12},{12,8},{16,20},{20,16},{24,28},{28,24},{32,36},... | collective-permute-start | bytes 589832 | tf_op jit(solution)/shard_map/ppermute | solution.py:316
  66.6 9.4 %copy-start.14 = (f32[384]{0:T(512)S(1)}, f32[384]{0:T(512)}, u32[]{:S(2)}) copy-start(f32[384]{0:T(512)} %constant.13.clone) | copy-start | bytes 4612
  66.6 14.4 %collective-permute-start.19 = (f32[64,512]{1,0:T(8,128)}, f32[64,512]{1,0:T(8,128)S(1)}, u32[]{:S(2)}, u32[]{:S(2)}) collective-permute-start(f32[64,512]{1,0:T(8,128)} %get-tuple-element.36), channel_id=1, source_target_pairs={{0,4},{4,8},{8,12},{12,16},{16,20},{20,24},{24,28},{28,32},{32,36}... | collective-permute-start | bytes 393224 | tf_op jit(solution)/shard_map/ppermute | solution.py:313
  76.0 7.9 %collective-permute-start.20 = (f32[64,512]{1,0:T(8,128)}, f32[64,512]{1,0:T(8,128)S(1)}, u32[]{:S(2)}, u32[]{:S(2)}) collective-permute-start(f32[64,512]{1,0:T(8,128)} %get-tuple-element.37), channel_id=1, source_target_pairs={{0,252},{4,0},{8,4},{12,8},{16,12},{20,16},{24,20},{28,24},{32,28}... | collective-permute-start | bytes 393224 | tf_op jit(solution)/shard_map/ppermute | solution.py:313
  (14 other events, 44.1 us)
where the time goes:
time: 86.9 us; the launch traced here: 85.5 us
  starting transfers between devices  34.6 us (40%)
  Pallas kernels  27.4 us (32%)
  waiting for transfers between devices  15.4 us (18%)
  local copies, waits for them, and re-layouts  4.08 us (5%)
  other arithmetic  2.51 us (3%)
  between operations  1.5 us (2%)
    ppermute x11, starting transfers between devices, swap(): return lax.ppermute(v, 'space', [(i, i ^ mask) for i in range(n_space)])  15.7 us
    ppermute x4, starting transfers between devices, shift(): lax.ppermute(v, 'space', [(i, (i + d) % n_space) for i in range(n_space)])  12.1 us
    ppermute x4, waiting for transfers between devices, shift(): lax.ppermute(v, 'space', [(i, (i + d) % n_space) for i in range(n_space)])  8.5 us
    pallas_call x1, Pallas kernels, shards(): call(forward_kernel, tuple([shape(ROWS, LAYER)] * 4), 1, 4, [pltpu.VMEM((...  7.59 us
    ppermute x11, waiting for transfers between devices, swap(): return lax.ppermute(v, 'space', [(i, i ^ mask) for i in range(n_space)])  6.87 us
    ppermute x6, starting transfers between devices, chan_swap(): return lax.ppermute(v, 'chan', [(i, i ^ mask) for i in range(4)])  6.83 us
    pallas_call x1, Pallas kernels, shards(): call(backward_kernel, tuple([shape(ROWS, LAYER)] * 3), 1, 8, [pltpu.VMEM(...  6.59 us
    pallas_call x1, Pallas kernels, shards(): call(structure_kernel, (shape(ROWS, 768), shape(ROWS, 768), shape(ROWS, L...  4.55 us
  transfers between devices with their start and end apart: 21, of which 6 were waited for; matrix products, arithmetic and copies ran while one was open for 3% of the time, Pallas kernels for 25%

commit v1 on v0

--- a/solution.py
+++ b/solution.py
@@ -14,11 +14,11 @@
 HALF = 384
 ROWS = 64
 PACK = 72
-CHUNK = 32
+FACTOR = math.sqrt(3.0 / 32768.0)
 LOG2E = math.log2(math.e)
 SCALE = 8.0 * LOG2E
 TERM = [0.3 * math.exp(-0.5 * (r - 3.5) ** 2) / SCALE**4 for r in range(NRAD)]
-VMEM_BYTES = 56 << 20
+VMEM_BYTES = 24 << 20
 
 
 vmem = pl.BlockSpec(memory_space=pltpu.VMEM)
@@ -30,10 +30,10 @@
 
 def half_space():
     m = np.arange(HALF)
-    nz = (m + 4) % 9 - 4
-    rest = (m - nz) // 9
-    ny = (rest + 4) % 9 - 4
-    nx = (rest - ny) // 9
+    plane = np.where(m < 360, m % 40 + 1, 0)
+    ny = (plane + 4) % 9 - 4
+    nx = (plane - ny) // 9
+    nz = np.where(m < 360, m // 40 - 4, m - 359)
     return nx, ny, nz
 
 
@@ -47,12 +47,12 @@
 
 
 def shape(*dims, dtype=f32):
-    return jax.ShapeDtypeStruct(dims, dtype)
-
-
-def call(kernel, out, n_smem, n_vmem, scratch=()):
+    return pltpu.VMEM(dims, dtype)
+
+
+def call(kernel, out, n_smem, n_vmem, scratch=(), far=()):
     many = isinstance(out, tuple)
-    return pl.pallas_call(
+    run = pl.pallas_call(
         kernel,
         out_shape=out,
         in_specs=[smem] * n_smem + [vmem] * n_vmem,
@@ -61,6 +61,14 @@
         compiler_params=pltpu.CompilerParams(vmem_limit_bytes=VMEM_BYTES),
     )
 
+    def place(*operands):
+        put = pltpu.with_memory_space_constraint
+        return run(
+            *[put(v, pltpu.HBM if k < n_smem or k in far else pltpu.VMEM) for k, v in enumerate(operands)]
+        )
+
+    return place
+
 
 def live_row(counts):
     lane = lax.broadcasted_iota(jnp.int32, (1, LAYER), 1)
@@ -75,16 +83,43 @@
     packed[ROWS + 3 : PACK, :] = jnp.broadcast_to(live, (PACK - ROWS - 3, LAYER))
 
 
-def filter_kernel(filters, forward, backward):
-    scaled = jnp.concatenate([filters[r] * TERM[r] for r in range(NRAD)], 0)
-    high, low = split(scaled)
-    backward[:, 0:256] = high
-    backward[:, 256:512] = high
-    backward[:, 512:768] = low
-    high, low = split(scaled.T)
-    forward[:, 0:512] = high
-    forward[:, 512:1024] = low
-    forward[:, 1024:1536] = high
+def forward_filter_kernel(filters, forward):
+    for r in range(0, NRAD, 2):
+        pair = jnp.concatenate([filters[r] * TERM[r], filters[r + 1] * TERM[r + 1]], 0)
+        high, low = split(pair.T)
+        for k in range(2):
+            lanes = slice(ROWS * k, ROWS * k + ROWS)
+            both_high = jnp.concatenate([high[:, lanes]] * 2, 1)
+            both_low = jnp.concatenate([low[:, lanes]] * 2, 1)
+            at = 128 * (r + k)
+            forward[:, at : at + 128] = both_high
+            forward[:, 1024 + at : 1024 + at + 128] = both_low
+            forward[:, 2048 + at : 2048 + at + 128] = both_high
+
+
+def backward_filter_kernel(filters, wavevectors, screened, backward, weights):
+    for r in range(NRAD):
+        rows = slice(ROWS * r, ROWS * r + ROWS)
+        high, low = split(filters[r] * TERM[r])
+        backward[rows, 0:256] = high
+        backward[rows, 256:512] = high
+        backward[rows, 512:768] = low
+    plane, nz = 9 * wavevectors[0:1, :] + wavevectors[1:2, :], wavevectors[2:3, :]
+    nz = jnp.where(plane < 0, -nz, nz)
+    plane = jnp.abs(plane)
+    code = jnp.where(plane > 0, 40 * (nz + 4) + plane - 1, 359 + jnp.abs(nz)).astype(f32)
+    column = jnp.broadcast_to(code, (8, LAYER)).T[:, 0:1]
+    lane = lax.broadcasted_iota(jnp.int32, (1, HALF), 1).astype(f32)
+    copies = jnp.zeros((8, HALF), f32)
+    for first in range(0, LAYER, 64):
+        hit = jnp.where(column[first : first + 64] == lane, 1.0, 0.0)
+        for k in range(0, 64, 8):
+            copies = copies + hit[k : k + 8]
+    copies = jnp.sum(copies, 0, keepdims=True)
+    value = copies * screened[0:1, :]
+    norm = jnp.sum(value * screened[0:1, :], 1, keepdims=True)
+    value = value * (FACTOR / jnp.sqrt(norm))
+    weights[...] = jnp.concatenate([value, value], 1)
 
 
 def trig(turns):
@@ -102,21 +137,22 @@
     row_y = packed[ROWS + 1 : ROWS + 2, :] * 0.5
     row_z = packed[ROWS + 2 : ROWS + 3, :]
 
-    def chunk(step, carry):
-        first = pl.multiple_of(step * CHUNK, CHUNK)
-        rows = pl.ds(first, CHUNK)
-        later = pl.ds(first + HALF, CHUNK)
-        turns = digits[rows, 0:1] * row_x + digits[rows, 1:2] * row_y + digits[rows, 2:3] * row_z
-        cos, sin = trig(turns)
-        high, low = split(cos)
-        table_high[rows, :] = high
-        table_low[rows, :] = low
-        high, low = split(sin)
-        table_high[later, :] = high
-        table_low[later, :] = low
-        return carry
-
-    lax.fori_loop(0, HALF // CHUNK, chunk, 0)
+    def put(at, cos, sin):
+        for base, value in ((at, cos), (HALF + at, sin)):
+            high, low = split(value)
+            table_high[base : base + value.shape[0], :] = high
+            table_low[base : base + value.shape[0], :] = low
+
+    tall = lax.broadcasted_iota(jnp.int32, (24, 1), 0).astype(f32) + 1.0
+    cos_z, sin_z = trig(tall * row_z)
+    put(360, cos_z, sin_z)
+    cos_p, sin_p = trig(digits[0:40, 0:1] * row_x + digits[0:40, 1:2] * row_y)
+    put(160, cos_p, sin_p)
+    for n in range(1, 5):
+        c, s = cos_z[n - 1 : n, :], sin_z[n - 1 : n, :]
+        cc, ss, sc, cs = cos_p * c, sin_p * s, sin_p * c, cos_p * s
+        put(160 + 40 * n, cc - ss, sc + cs)
+        put(160 - 40 * n, cc + ss, sc - cs)
     masked_high, masked_low = split(packed[0:ROWS, :])
     cot = cotangent[...] * packed[ROWS + 3 : ROWS + 4, :]
     cot_masked[...] = cot
@@ -213,19 +249,19 @@
             lows[128 * r : 128 * r + 128, :] = low
 
     visit(neighbours, amounts, columns, lines, flush, store)
-    lane = lax.broadcasted_iota(jnp.int32, (128, 128), 1)
-    for where in range(4):
-        pieces = []
-        for r in range(0, NRAD, 2):
-            even = sums[where * 1024 + 128 * r : where * 1024 + 128 * r + 128, :]
-            odd = sums[where * 1024 + 128 * r + 128 : where * 1024 + 128 * r + 256, :]
-            pieces.append(
-                jnp.where(lane < ROWS, even, odd)
-                + jnp.where(lane < ROWS, pltpu.roll(even, ROWS, 1), pltpu.roll(odd, ROWS, 1))
+    for pair in range(2):
+        wheres = (2 * pair, 2 * pair + 1)
+        first, second = [], []
+        for r in range(NRAD):
+            piece = jnp.concatenate(
+                [sums[1024 * w + 128 * r : 1024 * w + 128 * r + 128, :] for w in wheres], 0
             )
-        first, second = zip(*[split(p) for p in pieces])
-        right = jnp.concatenate([*first, *first, *second], 1)
-        share[:, 128 * where : 128 * where + 128] = dot(filters[...], right, NT)
+            high, low = split(piece)
+            first.append(high)
+            second.append(low)
+        share[:, 256 * pair : 256 * pair + 256] = dot(
+            filters[...], jnp.concatenate([*first, *first, *second], 1), NT
+        )
     for out, flip in ((own_panel, 0), (third_panel, 3), (near_panel, 1), (far_panel, 2)):
         out[...] = share[pl.ds(pl.multiple_of(ROWS * jnp.bitwise_xor(mine, flip), ROWS), ROWS), :]
 
@@ -277,33 +313,28 @@
             out[:, 128 * side : 128 * side + 128] = sums[at : at + ROWS, :] + sums[at + ROWS : at + 128, :]
 
 
-def project_kernel(mine_half, other_half, weights, table_high, table_low, packed, activated, cot_masked, middle,
+def project_kernel(mine, one, two, three, weights, table_high, table_low, packed, activated, cot_masked, middle,
                    updated, partial, scratch):
     space = lax.axis_index("space")
     core, x = space % 2, (space // 2) % 4
-    for half, at in ((mine_half, core), (other_half, 1 - core)):
-        scaled = half[...] * weights[...]
-        for d in range(4):
+    for d, piece in enumerate((mine, one, two, three)):
+        first, second = split(piece[...] * weights[...])
+        for half, at in ((0, core), (1, 1 - core)):
+            rows = slice(16 * half, 16 * half + 16)
             place = at * ROWS + 16 * jnp.bitwise_xor(x, d)
-            first, second = split(scaled[16 * d : 16 * d + 16])
-            scratch[pl.ds(pl.multiple_of(place, 16), 16), :] = first
-            scratch[pl.ds(pl.multiple_of(place + 128, 16), 16), :] = second
+            scratch[pl.ds(pl.multiple_of(place, 16), 16), :] = first[rows]
+            scratch[pl.ds(pl.multiple_of(place + 128, 16), 16), :] = second[rows]
     both = dot(scratch[...], table_high[...]) + dot(scratch[...], table_low[...])
     live = packed[ROWS + 3 : ROWS + 4, :]
     updated[...] = live * (packed[0:ROWS, :] + activated[...] + (both[:ROWS] + both[128 : 128 + ROWS]))
     partial[...] = live * (cot_masked[...] + middle[...] + (both[ROWS:128] + both[128 + ROWS :]))
 
 
-def wave_weights(wavevectors, n_space, slots):
-    code = jnp.abs(81 * wavevectors[0] + 9 * wavevectors[1] + wavevectors[2])
-    copies = jnp.sum((code[:, None] == jnp.arange(HALF)[None, :]).astype(f32), 0)
+def screening():
     nx, ny, nz = half_space()
     qx, qy, qz = 2 * math.pi / 64 * nx, math.pi * ny, 2 * math.pi * nz
     square = qx * qx + qy * qy + qz * qz
-    screened = jnp.asarray(np.exp(-square / 2000.0) / (square + 100.0), f32)
-    factor = math.sqrt(3.0 / (n_space * slots))
-    weights = factor * copies * screened / jnp.sqrt(jnp.sum(copies * screened * screened))
-    return jnp.concatenate([weights, weights])[None]
+    return np.tile((np.exp(-square / 2000.0) / (square + 100.0)).astype(np.float32), (8, 1))
 
 
 def shards(features, positions, counts, neighbours, wavevectors, filters, cotangent):
@@ -318,7 +349,7 @@
     def chan_swap(v, mask):
         return lax.ppermute(v, "chan", [(i, i ^ mask) for i in range(4)])
 
-    packed = call(pack_kernel, shape(PACK, LAYER), 1, 2)(counts, features, positions)
+    packed = call(pack_kernel, shape(PACK, LAYER), 1, 2, far=(1, 2))(counts, features, positions)
     below = shift(packed, 1)
     above = shift(packed, -1)
 
@@ -328,13 +359,9 @@
         structure_kernel,
         (shape(ROWS, 768), shape(ROWS, 768), shape(ROWS, LAYER),
          shape(768, LAYER, dtype=bf16), shape(768, LAYER, dtype=bf16)),
-        0, 3, [pltpu.VMEM((128, 768), f32)],
+        0, 3, [pltpu.VMEM((128, 768), f32)], far=(1, 2),
     )(packed, cotangent, jnp.asarray(digits))
-    forward_filters, backward_filters = call(
-        filter_kernel, (shape(256, 1536, dtype=bf16), shape(512, 768, dtype=bf16)), 0, 1
-    )(filters)
-    weights = wave_weights(wavevectors, n_space, LAYER)
-
+    forward_filters = call(forward_filter_kernel, shape(256, 3072, dtype=bf16), 0, 1, far=(0,))(filters)
     half = keep + swap(send, 1)
     got = []
     for d in (1, 2, 3):
@@ -356,20 +383,25 @@
     quarter = half[:16] + got[0] + got[1] + got[2]
     far = chan_swap(far_panel, 1)
     near = chan_swap(near_panel, 1)
-    quarter = quarter + swap(quarter, 32)
+    quarter = quarter + swap(quarter, 8)
     third_panel = third_panel + far
     third = chan_swap(third_panel, 3)
-    quarter = quarter + swap(quarter, 16)
+    quarter = quarter + swap(quarter, 32)
+    backward_filters, weights = call(
+        backward_filter_kernel, (shape(512, 768, dtype=bf16), shape(1, 768)), 0, 3,
+        far=(0, 1, 2),
+    )(filters, wavevectors, jnp.asarray(screening()))
     activated, upstream = call(
         activation_kernel, (shape(ROWS, LAYER), shape(ROWS, LAYER)), 0, 4
     )(own_panel, near, third, cot_masked)
     third_up = chan_swap(upstream, 3)
     near_up = chan_swap(upstream, 1)
-    quarter = quarter + swap(quarter, 8)
+    quarter = quarter + swap(quarter, 16)
     far_up = chan_swap(third_up, 1)
+    pair = jnp.concatenate([quarter, swap(quarter, 1)], 0)
     got = []
     for d in (1, 2, 3):
-        got.append(swap(quarter, 2 * d))
+        got.append(swap(pair, 2 * d))
     left, middle, right = call(
         backward_kernel, tuple([shape(ROWS, LAYER)] * 3), 1, 8,
         [
@@ -382,14 +414,12 @@
             pltpu.VMEM((1536, 128), f32),
         ],
     )(neighbours, packed, below, above, backward_filters, upstream, third_up, near_up, far_up)
-    half = jnp.concatenate([quarter, *got], 0)
     from_lower = shift(right, 1)
     from_upper = shift(left, -1)
-    other = swap(half, 1)
     updated, partial = call(
-        project_kernel, (shape(ROWS, LAYER), shape(ROWS, LAYER)), 0, 9,
+        project_kernel, (jax.ShapeDtypeStruct((ROWS, LAYER), f32), shape(ROWS, LAYER)), 0, 11,
         [pltpu.VMEM((256, 768), bf16)],
-    )(half, other, weights, table_high, table_low, packed, activated, cot_masked, middle)
+    )(pair, *got, weights, table_high, table_low, packed, activated, cot_masked, middle)
     grad_features = partial + packed[ROWS + 3][None] * (from_lower + from_upper)
     return updated, grad_features
 

time: 86.9 us -> 78.2 us (0.90)
  the two profiles are of different devices: /device:TPU:111 before, /device:TPU:4 now
where the time goes in v1:
time: 78.2 us; the launch traced here: 78 us
  starting transfers between devices  34.1 us (44%)
  Pallas kernels  25.1 us (32%)
  waiting for transfers between devices  17.2 us (22%)
  between operations  0.79 us (1%)
    pallas_call x8, Pallas kernels, place(): run(*[put(v, pltpu.HBM if k < n_smem or k in far else pltpu.VMEM) for k,...  25.1 us
    ppermute x11, starting transfers between devices, swap(): return lax.ppermute(v, 'space', [(i, i ^ mask) for i in range(n_space)])  21.4 us
    ppermute x11, waiting for transfers between devices, swap(): return lax.ppermute(v, 'space', [(i, i ^ mask) for i in range(n_space)])  13.4 us
    ppermute x6, starting transfers between devices, chan_swap(): return lax.ppermute(v, 'chan', [(i, i ^ mask) for i in range(4)])  9.16 us
    ppermute x6, waiting for transfers between devices, chan_swap(): return lax.ppermute(v, 'chan', [(i, i ^ mask) for i in range(4)])  3.74 us
    ppermute x4, starting transfers between devices, shift(): lax.ppermute(v, 'space', [(i, (i + d) % n_space) for i in range(n_space)])  3.63 us
  transfers between devices with their start and end apart: 21, of which 6 were waited for; matrix products, arithmetic and copies ran while one was open for 0% of the time, Pallas kernels for 31%

profile of v1, /device:TPU:4, one launch (start us, length us, event | category | flops | bytes accessed | tf_op | source)
XLA Modules:
  0.0 78.0 jit_solution(12325353134894855672)
XLA Ops:
  0.6 0.9 %shard_map.104.packed.own = f32[72,512]{1,0:T(8,128)S(1)} custom-call(s32[2]{0:T(128)} %counts.1, f32[64,512]{1,0:T(8,128)} %features.1, f32[3,512]{1,0:T(4,128)} %positions.1), custom_call_target="tpu_custom_call" | custom-call | tf_op jit(solution)/shard_map/pallas_call | solution.py:66
  1.7 1.7 %collective-permute-start.12 = (f32[72,512]{1,0:T(8,128)S(1)}, f32[72,512]{1,0:T(8,128)S(1)}, u32[]{:S(2)}, u32[]{:S(2)}) collective-permute-start(f32[72,512]{1,0:T(8,128)S(1)} %shard_map.104.packed.own), channel_id=1, source_target_pairs={{0,252},{4,0},{8,4},{12,8},{16,12},{20,16},{24,20},{28,24},{32,28}... | collective-permute-start | bytes 442376 | tf_op jit(solution)/shard_map/ppermute | solution.py:344
  3.4 2.0 %shard_map.105 = (f32[64,768]{1,0:T(8,128)S(1)}, f32[64,768]{1,0:T(8,128)S(1)}, f32[64,512]{1,0:T(8,128)S(1)}, bf16[768,512]{1,0:T(8,128)(2,1)S(1)}, bf16[768,512]{1,0:T(8,128)(2,1)S(1)}) custom-call(f32[72,512]{1,0:T(8,128)S(1)} %shard_map.104.packed.own, f32[64,512]{1,0:T(8,128)} %cotangent.1, f32[384,8]{1,0:T(8,128)} %constant.4.clone.digits), custom_call_target="tpu_custom_call" | custom-call | tf_op jit(solution)/shard_map/pallas_call | solution.py:66
  5.5 1.5 %shard_map.107.filters = bf16[256,3072]{1,0:T(8,128)(2,1)S(1)} custom-call(f32[8,64,256]{2,1,0:T(8,128)} %filters.3), custom_call_target="tpu_custom_call" | custom-call | tf_op jit(solution)/shard_map/pallas_call | solution.py:66
  7.0 9.2 %shard_map.108 = (f32[64,512]{1,0:T(8,128)S(1)}, f32[64,512]{1,0:T(8,128)S(1)}, f32[64,512]{1,0:T(8,128)S(1)}, f32[64,512]{1,0:T(8,128)S(1)}) custom-call(s32[2,4]{1,0:T(2,128)} %neighbours.3, f32[72,512]{1,0:T(8,128)S(1)} %shard_map.104.packed.own, f32[72,512]{1,0:T(8,128)S(1)} %collective-permute-done.11.below, ...), custom_call_target="tpu_custom_call" | custom-call | tf_op jit(solution)/shard_map/pallas_call | solution.py:66
  16.3 1.7 %collective-permute-start.14 = (f32[64,512]{1,0:T(8,128)S(1)}, f32[64,512]{1,0:T(8,128)S(1)}, u32[]{:S(2)}, u32[]{:S(2)}) collective-permute-start(f32[64,512]{1,0:T(8,128)S(1)} %get-tuple-element.28), channel_id=1, source_target_pairs={{0,1},{1,0},{2,3},{3,2},{4,5},{5,4},{6,7},{7,6},{8,9},{9,8},{10,11... | collective-permute-start | bytes 393224 | tf_op jit(solution)/shard_map/ppermute | solution.py:350
  18.4 3.7 %collective-permute-done.14 = f32[64,512]{1,0:T(8,128)S(1)} collective-permute-done((f32[64,512]{1,0:T(8,128)S(1)}, f32[64,512]{1,0:T(8,128)S(1)}, u32[]{:S(2)}, u32[]{:S(2)}) %collective-permute-start.14) | collective-permute-done | bytes 131104 | tf_op jit(solution)/shard_map/ppermute | solution.py:350
  22.2 3.1 %collective-permute-start.15 = (f32[64,512]{1,0:T(8,128)S(1)}, f32[64,512]{1,0:T(8,128)S(1)}, u32[]{:S(2)}, u32[]{:S(2)}) collective-permute-start(f32[64,512]{1,0:T(8,128)S(1)} %add.37), channel_id=1, source_target_pairs={{0,3},{1,2},{2,1},{3,0},{4,7},{5,6},{6,5},{7,4},{8,11},{9,10},{10,... | collective-permute-start | bytes 393224 | tf_op jit(solution)/shard_map/ppermute | solution.py:350
  25.4 3.9 %collective-permute-start.2 = (f32[16,768]{1,0:T(8,128)S(1)}, f32[16,768]{1,0:T(8,128)S(1)}, u32[]{:S(2)}, u32[]{:S(2)}) collective-permute-start(f32[16,768]{1,0:T(8,128)S(1)} %get-tuple-element.40), channel_id=1, source_target_pairs={{0,16},{4,20},{8,24},{12,28},{16,0},{20,4},{24,8},{28,12},{32,48},... | collective-permute-start | bytes 147464 | tf_op jit(solution)/shard_map/ppermute | solution.py:347
  29.9 1.9 %collective-permute-start.16 = (f32[64,512]{1,0:T(8,128)S(1)}, f32[64,512]{1,0:T(8,128)S(1)}, u32[]{:S(2)}, u32[]{:S(2)}) collective-permute-start(f32[64,512]{1,0:T(8,128)S(1)} %get-tuple-element.32.mine_up), channel_id=1, source_target_pairs={{0,3},{1,2},{2,1},{3,0},{4,7},{5,6},{6,5},{7,4},{8,11},{9,10},{10,... | collective-permute-start | bytes 393224 | tf_op jit(solution)/shard_map/ppermute | solution.py:350
  31.8 1.6 %collective-permute-done.3 = f32[16,768]{1,0:T(8,128)S(1)} collective-permute-done((f32[16,768]{1,0:T(8,128)S(1)}, f32[16,768]{1,0:T(8,128)S(1)}, u32[]{:S(2)}, u32[]{:S(2)}) %collective-permute-start.3) | collective-permute-done | bytes 49184 | tf_op jit(solution)/shard_map/ppermute | solution.py:347
  33.5 2.2 %collective-permute-start.4 = (f32[16,768]{1,0:T(8,128)S(1)}, f32[16,768]{1,0:T(8,128)S(1)}, u32[]{:S(2)}, u32[]{:S(2)}) collective-permute-start(f32[16,768]{1,0:T(8,128)S(1)} %fusion.1), channel_id=1, source_target_pairs={{0,32},{4,36},{8,40},{12,44},{16,48},{20,52},{24,56},{28,60},{32,0... | collective-permute-start | bytes 147464 | tf_op jit(solution)/shard_map/ppermute | solution.py:347
  35.6 2.1 %collective-permute-done.4 = f32[16,768]{1,0:T(8,128)S(1)} collective-permute-done((f32[16,768]{1,0:T(8,128)S(1)}, f32[16,768]{1,0:T(8,128)S(1)}, u32[]{:S(2)}, u32[]{:S(2)}) %collective-permute-start.4) | collective-permute-done | bytes 49184 | tf_op jit(solution)/shard_map/ppermute | solution.py:347
  37.7 6.6 %collective-permute-start.5 = (f32[16,768]{1,0:T(8,128)S(1)}, f32[16,768]{1,0:T(8,128)S(1)}, u32[]{:S(2)}, u32[]{:S(2)}) collective-permute-start(f32[16,768]{1,0:T(8,128)S(1)} %add.34), channel_id=1, source_target_pairs={{0,128},{4,132},{8,136},{12,140},{16,144},{20,148},{24,152},{28,15... | collective-permute-start | bytes 147464 | tf_op jit(solution)/shard_map/ppermute | solution.py:347
  44.5 1.9 %collective-permute-start.18 = (f32[64,512]{1,0:T(8,128)S(1)}, f32[64,512]{1,0:T(8,128)S(1)}, u32[]{:S(2)}, u32[]{:S(2)}) collective-permute-start(f32[64,512]{1,0:T(8,128)S(1)} %collective-permute-done.16.third_up), channel_id=1, source_target_pairs={{0,1},{1,0},{2,3},{3,2},{4,5},{5,4},{6,7},{7,6},{8,9},{9,8},{10,11... | collective-permute-start | bytes 393224 | tf_op jit(solution)/shard_map/ppermute | solution.py:350
  46.4 1.5 %collective-permute-start.6 = (f32[16,768]{1,0:T(8,128)S(1)}, f32[16,768]{1,0:T(8,128)S(1)}, u32[]{:S(2)}, u32[]{:S(2)}) collective-permute-start(f32[16,768]{1,0:T(8,128)S(1)} %add.35), channel_id=1, source_target_pairs={{0,64},{4,68},{8,72},{12,76},{16,80},{20,84},{24,88},{28,92},{32,9... | collective-permute-start | bytes 147464 | tf_op jit(solution)/shard_map/ppermute | solution.py:347
  47.9 3.6 %collective-permute-done.6 = f32[16,768]{1,0:T(8,128)S(1)} collective-permute-done((f32[16,768]{1,0:T(8,128)S(1)}, f32[16,768]{1,0:T(8,128)S(1)}, u32[]{:S(2)}, u32[]{:S(2)}) %collective-permute-start.6) | collective-permute-done | bytes 49184 | tf_op jit(solution)/shard_map/ppermute | solution.py:347
  51.8 1.5 %shard_map.106 = (bf16[512,768]{1,0:T(8,128)(2,1)S(1)}, f32[1,768]{1,0:T(1,128)S(1)}) custom-call(f32[8,64,256]{2,1,0:T(8,128)} %filters.3, s32[3,512]{1,0:T(4,128)} %wavevectors.1, f32[8,384]{1,0:T(8,128)} %constant.5.clone.screened), custom_call_target="tpu_custom_call" | custom-call | tf_op jit(solution)/shard_map/pallas_call | solution.py:66
  53.3 8.5 %shard_map.110 = (f32[64,512]{1,0:T(8,128)S(1)}, f32[64,512]{1,0:T(8,128)S(1)}, f32[64,512]{1,0:T(8,128)S(1)}) custom-call(s32[2,4]{1,0:T(2,128)} %neighbours.3, f32[72,512]{1,0:T(8,128)S(1)} %shard_map.104.packed.own, f32[72,512]{1,0:T(8,128)S(1)} %collective-permute-done.11.below, f32[72,512]{1,0:T(8,128)S(1)} %collective-permute-done.12.above, ...), custom_call_target="tpu_custom_call" | custom-call | tf_op jit(solution)/shard_map/pallas_call | solution.py:66
  61.9 1.7 %collective-permute-start.20 = (f32[64,512]{1,0:T(8,128)S(1)}, f32[64,512]{1,0:T(8,128)S(1)}, u32[]{:S(2)}, u32[]{:S(2)}) collective-permute-start(f32[64,512]{1,0:T(8,128)S(1)} %get-tuple-element.37), channel_id=1, source_target_pairs={{0,252},{4,0},{8,4},{12,8},{16,12},{20,16},{24,20},{28,24},{32,28}... | collective-permute-start | bytes 393224 | tf_op jit(solution)/shard_map/ppermute | solution.py:344
  63.8 6.1 %collective-permute-start.8 = (f32[32,768]{1,0:T(8,128)S(1)}, f32[32,768]{1,0:T(8,128)S(1)}, u32[]{:S(2)}, u32[]{:S(2)}) collective-permute-start(f32[32,768]{1,0:T(8,128)S(1)} %pad_maximum_fusion.mine), channel_id=1, source_target_pairs={{0,8},{4,12},{8,0},{12,4},{16,24},{20,28},{24,16},{28,20},{32,40},... | collective-permute-start | bytes 294920 | tf_op jit(solution)/shard_map/ppermute | solution.py:347
  69.9 2.6 %collective-permute-done.8.one = f32[32,768]{1,0:T(8,128)S(1)} collective-permute-done((f32[32,768]{1,0:T(8,128)S(1)}, f32[32,768]{1,0:T(8,128)S(1)}, u32[]{:S(2)}, u32[]{:S(2)}) %collective-permute-start.8) | collective-permute-done | bytes 98336 | tf_op jit(solution)/shard_map/ppermute | solution.py:347
  72.5 3.5 %collective-permute-done.9.two = f32[32,768]{1,0:T(8,128)S(1)} collective-permute-done((f32[32,768]{1,0:T(8,128)S(1)}, f32[32,768]{1,0:T(8,128)S(1)}, u32[]{:S(2)}, u32[]{:S(2)}) %collective-permute-start.9) | collective-permute-done | bytes 98336 | tf_op jit(solution)/shard_map/ppermute | solution.py:347
  76.0 1.3 %shard_map.111 = (f32[64,512]{1,0:T(8,128)}, f32[64,512]{1,0:T(8,128)S(1)}) custom-call(f32[32,768]{1,0:T(8,128)S(1)} %pad_maximum_fusion.mine, f32[32,768]{1,0:T(8,128)S(1)} %collective-permute-done.8.one, f32[32,768]{1,0:T(8,128)S(1)} %collective-permute-done.9.two, f32[32,768]{1,0:T(8,128)S(1)} %collective-permute-done.10.three, ...), custom_call_target="tpu_custom_call" | custom-call | tf_op jit(solution)/shard_map/pallas_call | solution.py:66
  (36 shorter events, 2.7 us)
Async XLA Ops:
  1.6 5.5 %collective-permute-start.11 = (f32[72,512]{1,0:T(8,128)S(1)}, f32[72,512]{1,0:T(8,128)S(1)}, u32[]{:S(2)}, u32[]{:S(2)}) collective-permute-start(f32[72,512]{1,0:T(8,128)S(1)} %shard_map.104.packed.own), channel_id=1, source_target_pairs={{0,4},{4,8},{8,12},{12,16},{16,20},{20,24},{24,28},{28,32},{32,36}... | collective-permute-start | bytes 442376 | tf_op jit(solution)/shard_map/ppermute | solution.py:344
  1.7 5.4 %collective-permute-start.12 = (f32[72,512]{1,0:T(8,128)S(1)}, f32[72,512]{1,0:T(8,128)S(1)}, u32[]{:S(2)}, u32[]{:S(2)}) collective-permute-start(f32[72,512]{1,0:T(8,128)S(1)} %shard_map.104.packed.own), channel_id=1, source_target_pairs={{0,252},{4,0},{8,4},{12,8},{16,12},{20,16},{24,20},{28,24},{32,28}... | collective-permute-start | bytes 442376 | tf_op jit(solution)/shard_map/ppermute | solution.py:344
  5.4 13.0 %collective-permute-start = (f32[64,768]{1,0:T(8,128)S(1)}, f32[64,768]{1,0:T(8,128)S(1)}, u32[]{:S(2)}, u32[]{:S(2)}) collective-permute-start(f32[64,768]{1,0:T(8,128)S(1)} %get-tuple-element.21), channel_id=1, source_target_pairs={{0,4},{4,0},{8,12},{12,8},{16,20},{20,16},{24,28},{28,24},{32,36},... | collective-permute-start | bytes 589832 | tf_op jit(solution)/shard_map/ppermute | solution.py:347
  16.3 5.9 %collective-permute-start.14 = (f32[64,512]{1,0:T(8,128)S(1)}, f32[64,512]{1,0:T(8,128)S(1)}, u32[]{:S(2)}, u32[]{:S(2)}) collective-permute-start(f32[64,512]{1,0:T(8,128)S(1)} %get-tuple-element.28), channel_id=1, source_target_pairs={{0,1},{1,0},{2,3},{3,2},{4,5},{5,4},{6,7},{7,6},{8,9},{9,8},{10,11... | collective-permute-start | bytes 393224 | tf_op jit(solution)/shard_map/ppermute | solution.py:350
  18.0 11.9 %collective-permute-start.13 = (f32[64,512]{1,0:T(8,128)S(1)}, f32[64,512]{1,0:T(8,128)S(1)}, u32[]{:S(2)}, u32[]{:S(2)}) collective-permute-start(f32[64,512]{1,0:T(8,128)S(1)} %get-tuple-element.26), channel_id=1, source_target_pairs={{0,1},{1,0},{2,3},{3,2},{4,5},{5,4},{6,7},{7,6},{8,9},{9,8},{10,11... | collective-permute-start | bytes 393224 | tf_op jit(solution)/shard_map/ppermute | solution.py:350
  22.2 7.6 %collective-permute-start.15 = (f32[64,512]{1,0:T(8,128)S(1)}, f32[64,512]{1,0:T(8,128)S(1)}, u32[]{:S(2)}, u32[]{:S(2)}) collective-permute-start(f32[64,512]{1,0:T(8,128)S(1)} %add.37), channel_id=1, source_target_pairs={{0,3},{1,2},{2,1},{3,0},{4,7},{5,6},{6,5},{7,4},{8,11},{9,10},{10,... | collective-permute-start | bytes 393224 | tf_op jit(solution)/shard_map/ppermute | solution.py:350
  25.3 6.5 %collective-permute-start.1 = (f32[16,768]{1,0:T(8,128)S(1)}, f32[16,768]{1,0:T(8,128)S(1)}, u32[]{:S(2)}, u32[]{:S(2)}) collective-permute-start(f32[16,768]{1,0:T(8,128)S(1)} %get-tuple-element.38), channel_id=1, source_target_pairs={{0,8},{4,12},{8,0},{12,4},{16,24},{20,28},{24,16},{28,20},{32,40},... | collective-permute-start | bytes 147464 | tf_op jit(solution)/shard_map/ppermute | solution.py:347
  25.4 6.4 %collective-permute-start.2 = (f32[16,768]{1,0:T(8,128)S(1)}, f32[16,768]{1,0:T(8,128)S(1)}, u32[]{:S(2)}, u32[]{:S(2)}) collective-permute-start(f32[16,768]{1,0:T(8,128)S(1)} %get-tuple-element.40), channel_id=1, source_target_pairs={{0,16},{4,20},{8,24},{12,28},{16,0},{20,4},{24,8},{28,12},{32,48},... | collective-permute-start | bytes 147464 | tf_op jit(solution)/shard_map/ppermute | solution.py:347
  29.4 4.1 %collective-permute-start.3 = (f32[16,768]{1,0:T(8,128)S(1)}, f32[16,768]{1,0:T(8,128)S(1)}, u32[]{:S(2)}, u32[]{:S(2)}) collective-permute-start(f32[16,768]{1,0:T(8,128)S(1)} %get-tuple-element.39), channel_id=1, source_target_pairs={{0,24},{4,28},{8,16},{12,20},{16,8},{20,12},{24,0},{28,4},{32,56},... | collective-permute-start | bytes 147464 | tf_op jit(solution)/shard_map/ppermute | solution.py:347
  29.9 14.6 %collective-permute-start.16 = (f32[64,512]{1,0:T(8,128)S(1)}, f32[64,512]{1,0:T(8,128)S(1)}, u32[]{:S(2)}, u32[]{:S(2)}) collective-permute-start(f32[64,512]{1,0:T(8,128)S(1)} %get-tuple-element.32.mine_up), channel_id=1, source_target_pairs={{0,3},{1,2},{2,1},{3,0},{4,7},{5,6},{6,5},{7,4},{8,11},{9,10},{10,... | collective-permute-start | bytes 393224 | tf_op jit(solution)/shard_map/ppermute | solution.py:350
  33.5 4.2 %collective-permute-start.4 = (f32[16,768]{1,0:T(8,128)S(1)}, f32[16,768]{1,0:T(8,128)S(1)}, u32[]{:S(2)}, u32[]{:S(2)}) collective-permute-start(f32[16,768]{1,0:T(8,128)S(1)} %fusion.1), channel_id=1, source_target_pairs={{0,32},{4,36},{8,40},{12,44},{16,48},{20,52},{24,56},{28,60},{32,0... | collective-permute-start | bytes 147464 | tf_op jit(solution)/shard_map/ppermute | solution.py:347
  37.7 8.7 %collective-permute-start.5 = (f32[16,768]{1,0:T(8,128)S(1)}, f32[16,768]{1,0:T(8,128)S(1)}, u32[]{:S(2)}, u32[]{:S(2)}) collective-permute-start(f32[16,768]{1,0:T(8,128)S(1)} %add.34), channel_id=1, source_target_pairs={{0,128},{4,132},{8,136},{12,140},{16,144},{20,148},{24,152},{28,15... | collective-permute-start | bytes 147464 | tf_op jit(solution)/shard_map/ppermute | solution.py:347
  44.3 8.9 %collective-permute-start.17 = (f32[64,512]{1,0:T(8,128)S(1)}, f32[64,512]{1,0:T(8,128)S(1)}, u32[]{:S(2)}, u32[]{:S(2)}) collective-permute-start(f32[64,512]{1,0:T(8,128)S(1)} %get-tuple-element.32.mine_up), channel_id=1, source_target_pairs={{0,1},{1,0},{2,3},{3,2},{4,5},{5,4},{6,7},{7,6},{8,9},{9,8},{10,11... | collective-permute-start | bytes 393224 | tf_op jit(solution)/shard_map/ppermute | solution.py:350
  44.5 8.8 %collective-permute-start.18 = (f32[64,512]{1,0:T(8,128)S(1)}, f32[64,512]{1,0:T(8,128)S(1)}, u32[]{:S(2)}, u32[]{:S(2)}) collective-permute-start(f32[64,512]{1,0:T(8,128)S(1)} %collective-permute-done.16.third_up), channel_id=1, source_target_pairs={{0,1},{1,0},{2,3},{3,2},{4,5},{5,4},{6,7},{7,6},{8,9},{9,8},{10,11... | collective-permute-start | bytes 393224 | tf_op jit(solution)/shard_map/ppermute | solution.py:350
  46.4 5.1 %collective-permute-start.6 = (f32[16,768]{1,0:T(8,128)S(1)}, f32[16,768]{1,0:T(8,128)S(1)}, u32[]{:S(2)}, u32[]{:S(2)}) collective-permute-start(f32[16,768]{1,0:T(8,128)S(1)} %add.35), channel_id=1, source_target_pairs={{0,64},{4,68},{8,72},{12,76},{16,80},{20,84},{24,88},{28,92},{32,9... | collective-permute-start | bytes 147464 | tf_op jit(solution)/shard_map/ppermute | solution.py:347
  51.5 12.2 %collective-permute-start.7 = (f32[16,768]{1,0:T(8,128)S(1)}, f32[16,768]{1,0:T(8,128)S(1)}, u32[]{:S(2)}, u32[]{:S(2)}) collective-permute-start(f32[16,768]{1,0:T(8,128)S(1)} %add.36), channel_id=1, source_target_pairs={{0,4},{4,0},{8,12},{12,8},{16,20},{20,16},{24,28},{28,24},{32,36},... | collective-permute-start | bytes 147464 | tf_op jit(solution)/shard_map/ppermute | solution.py:347
  61.9 15.5 %collective-permute-start.19 = (f32[64,512]{1,0:T(8,128)S(1)}, f32[64,512]{1,0:T(8,128)S(1)}, u32[]{:S(2)}, u32[]{:S(2)}) collective-permute-start(f32[64,512]{1,0:T(8,128)S(1)} %get-tuple-element.36), channel_id=1, source_target_pairs={{0,4},{4,8},{8,12},{12,16},{16,20},{20,24},{24,28},{28,32},{32,36}... | collective-permute-start | bytes 393224 | tf_op jit(solution)/shard_map/ppermute | solution.py:344
  61.9 15.4 %collective-permute-start.20 = (f32[64,512]{1,0:T(8,128)S(1)}, f32[64,512]{1,0:T(8,128)S(1)}, u32[]{:S(2)}, u32[]{:S(2)}) collective-permute-start(f32[64,512]{1,0:T(8,128)S(1)} %get-tuple-element.37), channel_id=1, source_target_pairs={{0,252},{4,0},{8,4},{12,8},{16,12},{20,16},{24,20},{28,24},{32,28}... | collective-permute-start | bytes 393224 | tf_op jit(solution)/shard_map/ppermute | solution.py:344
  63.7 6.2 %collective-permute-start.10 = (f32[32,768]{1,0:T(8,128)S(1)}, f32[32,768]{1,0:T(8,128)S(1)}, u32[]{:S(2)}, u32[]{:S(2)}) collective-permute-start(f32[32,768]{1,0:T(8,128)S(1)} %pad_maximum_fusion.mine), channel_id=1, source_target_pairs={{0,24},{4,28},{8,16},{12,20},{16,8},{20,12},{24,0},{28,4},{32,56},... | collective-permute-start | bytes 294920 | tf_op jit(solution)/shard_map/ppermute | solution.py:347
  63.8 8.7 %collective-permute-start.8 = (f32[32,768]{1,0:T(8,128)S(1)}, f32[32,768]{1,0:T(8,128)S(1)}, u32[]{:S(2)}, u32[]{:S(2)}) collective-permute-start(f32[32,768]{1,0:T(8,128)S(1)} %pad_maximum_fusion.mine), channel_id=1, source_target_pairs={{0,8},{4,12},{8,0},{12,4},{16,24},{20,28},{24,16},{28,20},{32,40},... | collective-permute-start | bytes 294920 | tf_op jit(solution)/shard_map/ppermute | solution.py:347
  69.9 6.1 %collective-permute-start.9 = (f32[32,768]{1,0:T(8,128)S(1)}, f32[32,768]{1,0:T(8,128)S(1)}, u32[]{:S(2)}, u32[]{:S(2)}) collective-permute-start(f32[32,768]{1,0:T(8,128)S(1)} %pad_maximum_fusion.mine), channel_id=1, source_target_pairs={{0,16},{4,20},{8,24},{12,28},{16,0},{20,4},{24,8},{28,12},{32,48},... | collective-permute-start | bytes 294920 | tf_op jit(solution)/shard_map/ppermute | solution.py:347

commit v2 on v1

--- a/solution.py
+++ b/solution.py
@@ -9,6 +9,7 @@
 from jax.sharding import PartitionSpec as P
 
 NRAD = 8
+NB = 4
 CAP = 256
 LAYER = 512
 HALF = 384
@@ -84,17 +85,11 @@
 
 
 def forward_filter_kernel(filters, forward):
-    for r in range(0, NRAD, 2):
-        pair = jnp.concatenate([filters[r] * TERM[r], filters[r + 1] * TERM[r + 1]], 0)
-        high, low = split(pair.T)
-        for k in range(2):
-            lanes = slice(ROWS * k, ROWS * k + ROWS)
-            both_high = jnp.concatenate([high[:, lanes]] * 2, 1)
-            both_low = jnp.concatenate([low[:, lanes]] * 2, 1)
-            at = 128 * (r + k)
-            forward[:, at : at + 128] = both_high
-            forward[:, 1024 + at : 1024 + at + 128] = both_low
-            forward[:, 2048 + at : 2048 + at + 128] = both_high
+    scaled = jnp.concatenate([filters[r] * TERM[r] for r in range(NRAD)], 0)
+    high, low = split(scaled.T)
+    forward[:, 0:512] = high
+    forward[:, 512:1024] = low
+    forward[:, 1024:1536] = high
 
 
 def backward_filter_kernel(filters, wavevectors, screened, backward, weights):
@@ -184,86 +179,102 @@
     return terms
 
 
-def layer_setup(sources, columns, lines, amounts):
-    own = sources[1]
-    flipped = own[ROWS:PACK, :].T * SCALE
-    for a in range(3):
-        columns[a] = jnp.broadcast_to(flipped[:, a : a + 1], (LAYER, 128))
+def store_terms(tiles, col, row):
+    for r, term in enumerate(radial_terms(col, row)):
+        high, low = split(term)
+        tiles[256 * r : 256 * r + 128, :] = high
+        tiles[256 * r + 128 : 256 * r + 256, :] = low
+
+
+def count_live(sources, amounts):
     for section, source in enumerate(sources):
         for side in range(2):
             lanes = slice(side * CAP, (side + 1) * CAP)
             amounts[2 * section + side] = jnp.sum(source[ROWS + 3 : ROWS + 4, lanes]).astype(jnp.int32)
-        for side in range(4):
-            for a in range(3):
-                at = slice(ROWS + a, ROWS + a + 1)
-                shift = (section - 1.0) * SCALE if a == 0 else 0.0
-                lines[4 * section + side, a : a + 1, :] = source[at, 128 * side : 128 * side + 128] * SCALE + shift
-
-
-def visit(neighbours, amounts, columns, lines, flush, store):
-    def outer(index, carry):
-        block, entry, side = index // 8, (index // 2) % 4, index % 2
-        chosen = neighbours[block, entry]
-        piece = 2 * chosen + side
-        trips = jnp.where(side * 128 < amounts[chosen], (amounts[2 + block] + 127) // 128, 0)
-
-        def inner(step, last):
-            flush(*last)
-            where = 2 * block + step
-            at = pl.ds(pl.multiple_of(where * 128, 128), 128)
-            col = [columns[a, at, :] for a in range(3)]
-            row = [lines[piece, a : a + 1, :] for a in range(3)]
-            store(radial_terms(col, row))
-            return where, piece
-
-        return lax.fori_loop(0, trips, inner, carry)
-
-    flush(*lax.fori_loop(0, 16, outer, (jnp.int32(0), jnp.int32(0))))
-
-
-def forward_kernel(neighbours, own, below, above, filters, own_panel, third_panel, near_panel, far_panel,
-                   columns, lines, amounts, values, highs, lows, sums, share):
-    mine = lax.axis_index("chan")
-    layer_setup((below, own, above), columns, lines, amounts)
-    for section, source in enumerate((below, own, above)):
+
+
+def list_live(block, neighbours, amounts, pieces):
+    def gather(index, found):
+        chosen, side = neighbours[block, index // 2], index % 2
+        pieces[found] = 2 * chosen + side
+        return found + jnp.where(side * 128 < amounts[chosen], 1, 0)
+
+    found = lax.fori_loop(0, 2 * NB, gather, jnp.int32(0))
+    pieces[found] = 12
+    return found
+
+
+def forward_setup(sources, places, values):
+    for section, source in enumerate(sources):
+        at = slice(section * LAYER, (section + 1) * LAYER)
+        flipped = source[ROWS:PACK, :].T * SCALE
+        lane = lax.broadcasted_iota(jnp.int32, (LAYER, 8), 1)
+        places[at, :] = flipped + jnp.where(lane == 0, (section - 1.0) * SCALE, 0.0)
         high, low = split(source[0:ROWS, :])
         for side in range(4):
             values[4 * section + side, 0:ROWS, :] = high[:, 128 * side : 128 * side + 128]
             values[4 * section + side, ROWS:128, :] = low[:, 128 * side : 128 * side + 128]
+    places[3 * LAYER :, :] = jnp.zeros((128, 8), f32)
+
+
+def forward_block(block, neighbours, sources, filters, out, places, values,
+                  amounts, pieces, columns, left, right, sums):
+    own = sources[1]
+    count_live(sources, amounts)
     sums[...] = jnp.zeros_like(sums)
-    highs[...] = jnp.zeros_like(highs)
-    lows[...] = jnp.zeros_like(lows)
-
-    def flush(where, piece):
+    lines = [
+        [own[ROWS + a : ROWS + a + 1, block * CAP + 128 * k : block * CAP + 128 * k + 128] * SCALE for a in range(3)]
+        for k in range(2)
+    ]
+    found = list_live(block, neighbours, amounts, pieces)
+
+    def spread(piece):
+        at = pl.ds(pl.multiple_of(piece * 128, 128), 128)
+        for a in range(3):
+            columns[a] = jnp.broadcast_to(places[at, a : a + 1], (128, 128))
+
+    def flush(piece):
         value = values[piece]
-        out = dot(
-            jnp.concatenate([highs[...], lows[...]], 1), jnp.concatenate([value, value], 1), NT
-        )
-        rows = pl.ds(pl.multiple_of(where * 1024, 1024), 1024)
-        sums[rows, :] = sums[rows, :] + out
-
-    def store(terms):
-        for r, term in enumerate(terms):
-            high, low = split(term)
-            highs[128 * r : 128 * r + 128, :] = high
-            lows[128 * r : 128 * r + 128, :] = low
-
-    visit(neighbours, amounts, columns, lines, flush, store)
-    for pair in range(2):
-        wheres = (2 * pair, 2 * pair + 1)
-        first, second = [], []
+        value = jnp.concatenate([value, value], 1)
         for r in range(NRAD):
-            piece = jnp.concatenate(
-                [sums[1024 * w + 128 * r : 1024 * w + 128 * r + 128, :] for w in wheres], 0
-            )
-            high, low = split(piece)
-            first.append(high)
-            second.append(low)
-        share[:, 256 * pair : 256 * pair + 256] = dot(
-            filters[...], jnp.concatenate([*first, *first, *second], 1), NT
-        )
+            rows = slice(256 * r, 256 * r + 256)
+            at = slice(128 * r, 128 * r + 128)
+            sums[at, :] = sums[at, :] + dot(value, jnp.concatenate([left[rows, :], right[rows, :]], 1))
+
+    def fill(index):
+        col = [columns[a] for a in range(3)]
+        for tiles, line in ((left, lines[0]), (right, lines[1])):
+            store_terms(tiles, col, line)
+        spread(pieces[index + 1])
+        return pieces[index]
+
+    def step(index, last):
+        flush(last)
+        return fill(index)
+
+    spread(pieces[0])
+    flush(lax.fori_loop(1, found, step, fill(0)))
+    first, second = [], []
+    for r in range(NRAD):
+        high, low = split(sums[128 * r : 128 * r + ROWS, :] + sums[128 * r + ROWS : 128 * r + 128, :])
+        first.append(high)
+        second.append(low)
+    out[...] = dot(filters[...], jnp.concatenate([*first, *first, *second], 0))
+
+
+def forward_first_kernel(neighbours, own, below, above, filters, share, places, values, *scratch):
+    forward_setup((below, own, above), places, values)
+    forward_block(0, neighbours, (below, own, above), filters, share, places, values, *scratch)
+
+
+def forward_second_kernel(neighbours, own, below, above, filters, other, places, values,
+                          own_panel, third_panel, near_panel, far_panel, share, *scratch):
+    mine = lax.axis_index("chan")
+    forward_block(1, neighbours, (below, own, above), filters, share, places, values, *scratch)
     for out, flip in ((own_panel, 0), (third_panel, 3), (near_panel, 1), (far_panel, 2)):
-        out[...] = share[pl.ds(pl.multiple_of(ROWS * jnp.bitwise_xor(mine, flip), ROWS), ROWS), :]
+        rows = pl.ds(pl.multiple_of(ROWS * jnp.bitwise_xor(mine, flip), ROWS), ROWS)
+        out[:, 0:CAP] = other[rows, :]
+        out[:, CAP:LAYER] = share[rows, :]
 
 
 def activation_kernel(own_panel, near, third, cot_masked, activated, upstream):
@@ -274,9 +285,10 @@
 
 
 def backward_kernel(neighbours, own, below, above, filters, mine_up, third_up, near_up, far_up,
-                    left, middle, right, columns, lines, amounts, panels, cots, tiles, sums):
+                    low_side, middle, high_side, columns, lines, amounts, pieces, panels, cots, left, right, sums):
     mine = lax.axis_index("chan")
-    layer_setup((below, own, above), columns, lines, amounts)
+    sources = (below, own, above)
+    count_live(sources, amounts)
     ups = [mine_up[...], third_up[...], near_up[...], far_up[...]]
     for value, flip in zip(ups, (0, 3, 1, 2)):
         first, second = split(value)
@@ -284,6 +296,16 @@
         panels[pl.ds(pl.multiple_of(at, ROWS), ROWS), :] = first
         panels[pl.ds(pl.multiple_of(at + 256, ROWS), ROWS), :] = second
         panels[pl.ds(pl.multiple_of(at + 512, ROWS), ROWS), :] = first
+    flipped = own[ROWS:PACK, :].T * SCALE
+    for a in range(3):
+        columns[a] = jnp.broadcast_to(flipped[:, a : a + 1], (LAYER, 128))
+    for section, source in enumerate(sources):
+        for side in range(4):
+            for a in range(3):
+                at = slice(ROWS + a, ROWS + a + 1)
+                shift = (section - 1.0) * SCALE if a == 0 else 0.0
+                lines[4 * section + side, a : a + 1, :] = source[at, 128 * side : 128 * side + 128] * SCALE + shift
+    lines[12] = jnp.full((8, 128), 1e4, f32)
     cot = dot(filters[...], panels[...])
     for r in range(NRAD):
         first, second = split(cot[ROWS * r : ROWS * r + ROWS])
@@ -291,23 +313,40 @@
             cots[NRAD * where + r, 0:ROWS, :] = first[:, 128 * where : 128 * where + 128]
             cots[NRAD * where + r, ROWS:128, :] = second[:, 128 * where : 128 * where + 128]
     sums[...] = jnp.zeros_like(sums)
-    tiles[...] = jnp.zeros_like(tiles)
-
-    def flush(where, piece):
+
+    def flush(where, one, two):
         parts = []
         for r in range(NRAD):
             parts += [cots[NRAD * where + r]] * 2
-        rows = pl.ds(pl.multiple_of(piece * 128, 128), 128)
-        sums[rows, :] = sums[rows, :] + dot(jnp.concatenate(parts, 1), tiles[...])
-
-    def store(terms):
-        for r, term in enumerate(terms):
-            high, low = split(term)
-            tiles[256 * r : 256 * r + 128, :] = high
-            tiles[256 * r + 128 : 256 * r + 256, :] = low
-
-    visit(neighbours, amounts, columns, lines, flush, store)
-    for section, out in enumerate((left, middle, right)):
+        out = dot(jnp.concatenate(parts, 1), jnp.concatenate([left[...], right[...]], 1))
+        for piece, lanes in ((one, slice(0, 128)), (two, slice(128, 256))):
+            rows = pl.ds(pl.multiple_of(piece * 128, 128), 128)
+            sums[rows, :] = sums[rows, :] + out[:, lanes]
+
+    def fill(where, one, two):
+        at = pl.ds(pl.multiple_of(where * 128, 128), 128)
+        col = [columns[a, at, :] for a in range(3)]
+        for tiles, piece in ((left, one), (right, two)):
+            store_terms(tiles, col, [lines[piece, a : a + 1, :] for a in range(3)])
+        return where, one, two
+
+    carry = None
+    for block in range(2):
+        found = list_live(block, neighbours, amounts, pieces)
+        pairs = (found + 1) // 2
+        total = pairs * ((amounts[2 + block] + 127) // 128)
+        if block == 0:
+            carry = fill(jnp.int32(0), pieces[0], pieces[1])
+
+        def step(index, last):
+            flush(*last)
+            half = jnp.where(index >= pairs, 1, 0)
+            pair = index - half * pairs
+            return fill(2 * block + half, pieces[2 * pair], pieces[2 * pair + 1])
+
+        carry = lax.fori_loop(1 - block, total, step, carry)
+    flush(*carry)
+    for section, out in enumerate((low_side, middle, high_side)):
         for side in range(4):
             at = 128 * (4 * section + side)
             out[:, 128 * side : 128 * side + 128] = sums[at : at + ROWS, :] + sums[at + ROWS : at + 128, :]
@@ -361,32 +400,37 @@
          shape(768, LAYER, dtype=bf16), shape(768, LAYER, dtype=bf16)),
         0, 3, [pltpu.VMEM((128, 768), f32)], far=(1, 2),
     )(packed, cotangent, jnp.asarray(digits))
-    forward_filters = call(forward_filter_kernel, shape(256, 3072, dtype=bf16), 0, 1, far=(0,))(filters)
+    forward_filters = call(forward_filter_kernel, shape(256, 1536, dtype=bf16), 0, 1, far=(0,))(filters)
     half = keep + swap(send, 1)
     got = []
     for d in (1, 2, 3):
         got.append(swap(half[16 * d : 16 * d + 16], 2 * d))
 
-    own_panel, third_panel, near_panel, far_panel = call(
-        forward_kernel, tuple([shape(ROWS, LAYER)] * 4), 1, 4,
-        [
-            pltpu.VMEM((3, LAYER, 128), f32),
-            pltpu.VMEM((12, 8, 128), f32),
-            pltpu.SMEM((6,), jnp.int32),
-            pltpu.VMEM((12, 128, 128), bf16),
-            pltpu.VMEM((1024, 128), bf16),
-            pltpu.VMEM((1024, 128), bf16),
-            pltpu.VMEM((4096, 128), f32),
-            pltpu.VMEM((256, LAYER), f32),
-        ],
+    scratch = [
+        pltpu.SMEM((6,), jnp.int32),
+        pltpu.SMEM((10,), jnp.int32),
+        pltpu.VMEM((3, 128, 128), f32),
+        pltpu.VMEM((2048, 128), bf16),
+        pltpu.VMEM((2048, 128), bf16),
+        pltpu.VMEM((1024, CAP), f32),
+    ]
+    share, places, values = call(
+        forward_first_kernel,
+        (shape(256, CAP), shape(3 * LAYER + 128, 8), shape(12, 128, 128, dtype=bf16)),
+        1, 4, scratch,
     )(neighbours, packed, below, above, forward_filters)
     quarter = half[:16] + got[0] + got[1] + got[2]
+    quarter = quarter + swap(quarter, 8)
+    own_panel, third_panel, near_panel, far_panel = call(
+        forward_second_kernel, tuple([shape(ROWS, LAYER)] * 4), 1, 7,
+        [pltpu.VMEM((256, CAP), f32), *scratch],
+    )(neighbours, packed, below, above, forward_filters, share, places, values)
     far = chan_swap(far_panel, 1)
     near = chan_swap(near_panel, 1)
-    quarter = quarter + swap(quarter, 8)
+    quarter = quarter + swap(quarter, 32)
     third_panel = third_panel + far
     third = chan_swap(third_panel, 3)
-    quarter = quarter + swap(quarter, 32)
+    quarter = quarter + swap(quarter, 16)
     backward_filters, weights = call(
         backward_filter_kernel, (shape(512, 768, dtype=bf16), shape(1, 768)), 0, 3,
         far=(0, 1, 2),
@@ -396,7 +440,6 @@
     )(own_panel, near, third, cot_masked)
     third_up = chan_swap(upstream, 3)
     near_up = chan_swap(upstream, 1)
-    quarter = quarter + swap(quarter, 16)
     far_up = chan_swap(third_up, 1)
     pair = jnp.concatenate([quarter, swap(quarter, 1)], 0)
     got = []
@@ -406,12 +449,14 @@
         backward_kernel, tuple([shape(ROWS, LAYER)] * 3), 1, 8,
         [
             pltpu.VMEM((3, LAYER, 128), f32),
-            pltpu.VMEM((12, 8, 128), f32),
+            pltpu.VMEM((13, 8, 128), f32),
             pltpu.SMEM((6,), jnp.int32),
+            pltpu.SMEM((10,), jnp.int32),
             pltpu.VMEM((768, LAYER), bf16),
             pltpu.VMEM((32, 128, 128), bf16),
             pltpu.VMEM((2048, 128), bf16),
-            pltpu.VMEM((1536, 128), f32),
+            pltpu.VMEM((2048, 128), bf16),
+            pltpu.VMEM((13 * 128, 128), f32),
         ],
     )(neighbours, packed, below, above, backward_filters, upstream, third_up, near_up, far_up)
     from_lower = shift(right, 1)

time: 78.2 us -> 78.8 us (level)
  waiting for transfers between devices: 17.2 us -> 23.2 us
  starting transfers between devices: 34.1 us -> 30.3 us
  Pallas kernels: 25.1 us -> 23.3 us
    ppermute x11, waiting for transfers between devices: 13.4 us -> 19.3 us  [swap(): return lax.ppermute(v, 'space', [(i, i ^ mask) for i in range(n_space)])]
    ppermute x11, starting transfers between devices: 21.4 us -> 18.9 us  [swap(): return lax.ppermute(v, 'space', [(i, i ^ mask) for i in range(n_space)])]
    pallas_call x8 -> x9, Pallas kernels: 25.1 us -> 23.3 us  [place(): run(*[put(v, pltpu.HBM if k < n_smem or k in far else pltpu.VMEM) for k,...]
    ppermute x6, starting transfers between devices: 9.16 us -> 7.77 us  [chan_swap(): return lax.ppermute(v, 'chan', [(i, i ^ mask) for i in range(4)])]
  transfers between devices with their start and end apart: 21 -> 21, of which waited for: 6 -> 8; matrix products, arithmetic and copies ran while one was open for 0% -> 0% of each run, Pallas kernels for 31% -> 29%
where the time goes in v2:
time: 78.8 us; the launch traced here: 78.5 us
  starting transfers between devices  30.3 us (38%)
  Pallas kernels  23.3 us (30%)
  waiting for transfers between devices  23.2 us (29%)
  between operations  0.81 us (1%)
    pallas_call x9, Pallas kernels, place(): run(*[put(v, pltpu.HBM if k < n_smem or k in far else pltpu.VMEM) for k,...  23.3 us
    ppermute x11, waiting for transfers between devices, swap(): return lax.ppermute(v, 'space', [(i, i ^ mask) for i in range(n_space)])  19.3 us
    ppermute x11, starting transfers between devices, swap(): return lax.ppermute(v, 'space', [(i, i ^ mask) for i in range(n_space)])  18.9 us
    ppermute x6, starting transfers between devices, chan_swap(): return lax.ppermute(v, 'chan', [(i, i ^ mask) for i in range(4)])  7.77 us
    ppermute x6, waiting for transfers between devices, chan_swap(): return lax.ppermute(v, 'chan', [(i, i ^ mask) for i in range(4)])  3.95 us
    ppermute x4, starting transfers between devices, shift(): lax.ppermute(v, 'space', [(i, (i + d) % n_space) for i in range(n_space)])  3.63 us
  transfers between devices with their start and end apart: 21, of which 8 were waited for; matrix products, arithmetic and copies ran while one was open for 0% of the time, Pallas kernels for 29%

profile of v2, /device:TPU:4, one launch (start us, length us, event | category | flops | bytes accessed | tf_op | source)
XLA Modules:
  0.0 78.5 jit_solution(4362780715543032819)
XLA Ops:
  0.6 0.9 %shard_map.104.packed.own = f32[72,512]{1,0:T(8,128)S(1)} custom-call(s32[2]{0:T(128)} %counts.1, f32[64,512]{1,0:T(8,128)} %features.1, f32[3,512]{1,0:T(4,128)} %positions.1), custom_call_target="tpu_custom_call" | custom-call | tf_op jit(solution)/shard_map/pallas_call | solution.py:67
  1.7 1.7 %collective-permute-start.12 = (f32[72,512]{1,0:T(8,128)S(1)}, f32[72,512]{1,0:T(8,128)S(1)}, u32[]{:S(2)}, u32[]{:S(2)}) collective-permute-start(f32[72,512]{1,0:T(8,128)S(1)} %shard_map.104.packed.own), channel_id=1, source_target_pairs={{0,252},{4,0},{8,4},{12,8},{16,12},{20,16},{24,20},{28,24},{32,28}... | collective-permute-start | bytes 442376 | tf_op jit(solution)/shard_map/ppermute | solution.py:383
  3.4 2.0 %shard_map.105 = (f32[64,768]{1,0:T(8,128)S(1)}, f32[64,768]{1,0:T(8,128)S(1)}, f32[64,512]{1,0:T(8,128)S(1)}, bf16[768,512]{1,0:T(8,128)(2,1)S(1)}, bf16[768,512]{1,0:T(8,128)(2,1)S(1)}) custom-call(f32[72,512]{1,0:T(8,128)S(1)} %shard_map.104.packed.own, f32[64,512]{1,0:T(8,128)} %cotangent.1, f32[384,8]{1,0:T(8,128)} %constant.4.clone.digits), custom_call_target="tpu_custom_call" | custom-call | tf_op jit(solution)/shard_map/pallas_call | solution.py:67
  5.5 1.3 %shard_map.107.filters = bf16[256,1536]{1,0:T(8,128)(2,1)S(1)} custom-call(f32[8,64,256]{2,1,0:T(8,128)} %filters.3), custom_call_target="tpu_custom_call" | custom-call | tf_op jit(solution)/shard_map/pallas_call | solution.py:67
  6.8 5.2 %shard_map.108 = (f32[256,256]{1,0:T(8,128)S(1)}, f32[1664,8]{1,0:T(8,128)S(1)}, bf16[12,128,128]{2,1,0:T(8,128)(2,1)S(1)}) custom-call(s32[2,4]{1,0:T(2,128)} %neighbours.5, f32[72,512]{1,0:T(8,128)S(1)} %shard_map.104.packed.own, f32[72,512]{1,0:T(8,128)S(1)} %collective-permute-done.11.below, f32[72,512]{1,0:T(8,128)S(1)} %collective-permute-done.12.above, ...), custom_call_target="tpu_custom_call" | custom-call | tf_op jit(solution)/shard_map/pallas_call | solution.py:67
  12.0 4.6 %shard_map.109 = (f32[64,512]{1,0:T(8,128)S(1)}, f32[64,512]{1,0:T(8,128)S(1)}, f32[64,512]{1,0:T(8,128)S(1)}, f32[64,512]{1,0:T(8,128)S(1)}) custom-call(s32[2,4]{1,0:T(2,128)} %neighbours.5, f32[72,512]{1,0:T(8,128)S(1)} %shard_map.104.packed.own, f32[72,512]{1,0:T(8,128)S(1)} %collective-permute-done.11.below, ...), custom_call_target="tpu_custom_call" | custom-call | tf_op jit(solution)/shard_map/pallas_call | solution.py:67
  16.6 1.7 %collective-permute-start.14 = (f32[64,512]{1,0:T(8,128)S(1)}, f32[64,512]{1,0:T(8,128)S(1)}, u32[]{:S(2)}, u32[]{:S(2)}) collective-permute-start(f32[64,512]{1,0:T(8,128)S(1)} %get-tuple-element.34), channel_id=1, source_target_pairs={{0,1},{1,0},{2,3},{3,2},{4,5},{5,4},{6,7},{7,6},{8,9},{9,8},{10,11... | collective-permute-start | bytes 393224 | tf_op jit(solution)/shard_map/ppermute | solution.py:389
  18.8 3.9 %collective-permute-done.14 = f32[64,512]{1,0:T(8,128)S(1)} collective-permute-done((f32[64,512]{1,0:T(8,128)S(1)}, f32[64,512]{1,0:T(8,128)S(1)}, u32[]{:S(2)}, u32[]{:S(2)}) %collective-permute-start.14) | collective-permute-done | bytes 131104 | tf_op jit(solution)/shard_map/ppermute | solution.py:389
  22.7 3.1 %collective-permute-start.15 = (f32[64,512]{1,0:T(8,128)S(1)}, f32[64,512]{1,0:T(8,128)S(1)}, u32[]{:S(2)}, u32[]{:S(2)}) collective-permute-start(f32[64,512]{1,0:T(8,128)S(1)} %add.37), channel_id=1, source_target_pairs={{0,3},{1,2},{2,1},{3,0},{4,7},{5,6},{6,5},{7,4},{8,11},{9,10},{10,... | collective-permute-start | bytes 393224 | tf_op jit(solution)/shard_map/ppermute | solution.py:389
  26.0 5.2 %collective-permute-start.2 = (f32[16,768]{1,0:T(8,128)S(1)}, f32[16,768]{1,0:T(8,128)S(1)}, u32[]{:S(2)}, u32[]{:S(2)}) collective-permute-start(f32[16,768]{1,0:T(8,128)S(1)} %get-tuple-element.46), channel_id=1, source_target_pairs={{0,16},{4,20},{8,24},{12,28},{16,0},{20,4},{24,8},{28,12},{32,48},... | collective-permute-start | bytes 147464 | tf_op jit(solution)/shard_map/ppermute | solution.py:386
  32.2 1.4 %collective-permute-done.2 = f32[16,768]{1,0:T(8,128)S(1)} collective-permute-done((f32[16,768]{1,0:T(8,128)S(1)}, f32[16,768]{1,0:T(8,128)S(1)}, u32[]{:S(2)}, u32[]{:S(2)}) %collective-permute-start.2) | collective-permute-done | bytes 49184 | tf_op jit(solution)/shard_map/ppermute | solution.py:386
  33.6 1.6 %collective-permute-done.3 = f32[16,768]{1,0:T(8,128)S(1)} collective-permute-done((f32[16,768]{1,0:T(8,128)S(1)}, f32[16,768]{1,0:T(8,128)S(1)}, u32[]{:S(2)}, u32[]{:S(2)}) %collective-permute-start.3) | collective-permute-done | bytes 49184 | tf_op jit(solution)/shard_map/ppermute | solution.py:386
  35.3 4.1 %collective-permute-done.4 = f32[16,768]{1,0:T(8,128)S(1)} collective-permute-done((f32[16,768]{1,0:T(8,128)S(1)}, f32[16,768]{1,0:T(8,128)S(1)}, u32[]{:S(2)}, u32[]{:S(2)}) %collective-permute-start.4) | collective-permute-done | bytes 49184 | tf_op jit(solution)/shard_map/ppermute | solution.py:386
  39.4 5.0 %collective-permute-start.5 = (f32[16,768]{1,0:T(8,128)S(1)}, f32[16,768]{1,0:T(8,128)S(1)}, u32[]{:S(2)}, u32[]{:S(2)}) collective-permute-start(f32[16,768]{1,0:T(8,128)S(1)} %add.34), channel_id=1, source_target_pairs={{0,128},{4,132},{8,136},{12,140},{16,144},{20,148},{24,152},{28,15... | collective-permute-start | bytes 147464 | tf_op jit(solution)/shard_map/ppermute | solution.py:386
  44.8 1.8 %collective-permute-start.18 = (f32[64,512]{1,0:T(8,128)S(1)}, f32[64,512]{1,0:T(8,128)S(1)}, u32[]{:S(2)}, u32[]{:S(2)}) collective-permute-start(f32[64,512]{1,0:T(8,128)S(1)} %collective-permute-done.16.third_up), channel_id=1, source_target_pairs={{0,1},{1,0},{2,3},{3,2},{4,5},{5,4},{6,7},{7,6},{8,9},{9,8},{10,11... | collective-permute-start | bytes 393224 | tf_op jit(solution)/shard_map/ppermute | solution.py:389
  46.5 1.4 %collective-permute-done.5 = f32[16,768]{1,0:T(8,128)S(1)} collective-permute-done((f32[16,768]{1,0:T(8,128)S(1)}, f32[16,768]{1,0:T(8,128)S(1)}, u32[]{:S(2)}, u32[]{:S(2)}) %collective-permute-start.5) | collective-permute-done | bytes 49184 | tf_op jit(solution)/shard_map/ppermute | solution.py:386
  48.4 4.6 %collective-permute-done.6 = f32[16,768]{1,0:T(8,128)S(1)} collective-permute-done((f32[16,768]{1,0:T(8,128)S(1)}, f32[16,768]{1,0:T(8,128)S(1)}, u32[]{:S(2)}, u32[]{:S(2)}) %collective-permute-start.6) | collective-permute-done | bytes 49184 | tf_op jit(solution)/shard_map/ppermute | solution.py:386
  53.1 1.5 %shard_map.106 = (bf16[512,768]{1,0:T(8,128)(2,1)S(1)}, f32[1,768]{1,0:T(1,128)S(1)}) custom-call(f32[8,64,256]{2,1,0:T(8,128)} %filters.3, s32[3,512]{1,0:T(4,128)} %wavevectors.1, f32[8,384]{1,0:T(8,128)} %constant.5.clone.screened), custom_call_target="tpu_custom_call" | custom-call | tf_op jit(solution)/shard_map/pallas_call | solution.py:67
  54.6 6.4 %shard_map.111 = (f32[64,512]{1,0:T(8,128)S(1)}, f32[64,512]{1,0:T(8,128)S(1)}, f32[64,512]{1,0:T(8,128)S(1)}) custom-call(s32[2,4]{1,0:T(2,128)} %neighbours.5, f32[72,512]{1,0:T(8,128)S(1)} %shard_map.104.packed.own, f32[72,512]{1,0:T(8,128)S(1)} %collective-permute-done.11.below, f32[72,512]{1,0:T(8,128)S(1)} %collective-permute-done.12.above, ...), custom_call_target="tpu_custom_call" | custom-call | tf_op jit(solution)/shard_map/pallas_call | solution.py:67
  61.2 1.7 %collective-permute-start.20 = (f32[64,512]{1,0:T(8,128)S(1)}, f32[64,512]{1,0:T(8,128)S(1)}, u32[]{:S(2)}, u32[]{:S(2)}) collective-permute-start(f32[64,512]{1,0:T(8,128)S(1)} %get-tuple-element.43), channel_id=1, source_target_pairs={{0,252},{4,0},{8,4},{12,8},{16,12},{20,16},{24,20},{28,24},{32,28}... | collective-permute-start | bytes 393224 | tf_op jit(solution)/shard_map/ppermute | solution.py:383
  63.0 7.4 %collective-permute-start.8 = (f32[32,768]{1,0:T(8,128)S(1)}, f32[32,768]{1,0:T(8,128)S(1)}, u32[]{:S(2)}, u32[]{:S(2)}) collective-permute-start(f32[32,768]{1,0:T(8,128)S(1)} %pad_maximum_fusion.mine), channel_id=1, source_target_pairs={{0,8},{4,12},{8,0},{12,4},{16,24},{20,28},{24,16},{28,20},{32,40},... | collective-permute-start | bytes 294920 | tf_op jit(solution)/shard_map/ppermute | solution.py:386
  70.4 2.6 %collective-permute-done.8.one = f32[32,768]{1,0:T(8,128)S(1)} collective-permute-done((f32[32,768]{1,0:T(8,128)S(1)}, f32[32,768]{1,0:T(8,128)S(1)}, u32[]{:S(2)}, u32[]{:S(2)}) %collective-permute-start.8) | collective-permute-done | bytes 98336 | tf_op jit(solution)/shard_map/ppermute | solution.py:386
  73.0 3.5 %collective-permute-done.9.two = f32[32,768]{1,0:T(8,128)S(1)} collective-permute-done((f32[32,768]{1,0:T(8,128)S(1)}, f32[32,768]{1,0:T(8,128)S(1)}, u32[]{:S(2)}, u32[]{:S(2)}) %collective-permute-start.9) | collective-permute-done | bytes 98336 | tf_op jit(solution)/shard_map/ppermute | solution.py:386
  76.5 1.3 %shard_map.112 = (f32[64,512]{1,0:T(8,128)}, f32[64,512]{1,0:T(8,128)S(1)}) custom-call(f32[32,768]{1,0:T(8,128)S(1)} %pad_maximum_fusion.mine, f32[32,768]{1,0:T(8,128)S(1)} %collective-permute-done.8.one, f32[32,768]{1,0:T(8,128)S(1)} %collective-permute-done.9.two, f32[32,768]{1,0:T(8,128)S(1)} %collective-permute-done.10.three, ...), custom_call_target="tpu_custom_call" | custom-call | tf_op jit(solution)/shard_map/pallas_call | solution.py:67
  (37 shorter events, 3.7 us)
Async XLA Ops:
  1.6 5.2 %collective-permute-start.11 = (f32[72,512]{1,0:T(8,128)S(1)}, f32[72,512]{1,0:T(8,128)S(1)}, u32[]{:S(2)}, u32[]{:S(2)}) collective-permute-start(f32[72,512]{1,0:T(8,128)S(1)} %shard_map.104.packed.own), channel_id=1, source_target_pairs={{0,4},{4,8},{8,12},{12,16},{16,20},{20,24},{24,28},{28,32},{32,36}... | collective-permute-start | bytes 442376 | tf_op jit(solution)/shard_map/ppermute | solution.py:383
  1.7 5.1 %collective-permute-start.12 = (f32[72,512]{1,0:T(8,128)S(1)}, f32[72,512]{1,0:T(8,128)S(1)}, u32[]{:S(2)}, u32[]{:S(2)}) collective-permute-start(f32[72,512]{1,0:T(8,128)S(1)} %shard_map.104.packed.own), channel_id=1, source_target_pairs={{0,252},{4,0},{8,4},{12,8},{16,12},{20,16},{24,20},{28,24},{32,28}... | collective-permute-start | bytes 442376 | tf_op jit(solution)/shard_map/ppermute | solution.py:383
  5.4 13.3 %collective-permute-start = (f32[64,768]{1,0:T(8,128)S(1)}, f32[64,768]{1,0:T(8,128)S(1)}, u32[]{:S(2)}, u32[]{:S(2)}) collective-permute-start(f32[64,768]{1,0:T(8,128)S(1)} %get-tuple-element.24), channel_id=1, source_target_pairs={{0,4},{4,0},{8,12},{12,8},{16,20},{20,16},{24,28},{28,24},{32,36},... | collective-permute-start | bytes 589832 | tf_op jit(solution)/shard_map/ppermute | solution.py:386
  16.6 6.1 %collective-permute-start.14 = (f32[64,512]{1,0:T(8,128)S(1)}, f32[64,512]{1,0:T(8,128)S(1)}, u32[]{:S(2)}, u32[]{:S(2)}) collective-permute-start(f32[64,512]{1,0:T(8,128)S(1)} %get-tuple-element.34), channel_id=1, source_target_pairs={{0,1},{1,0},{2,3},{3,2},{4,5},{5,4},{6,7},{7,6},{8,9},{9,8},{10,11... | collective-permute-start | bytes 393224 | tf_op jit(solution)/shard_map/ppermute | solution.py:389
  18.3 13.3 %collective-permute-start.13 = (f32[64,512]{1,0:T(8,128)S(1)}, f32[64,512]{1,0:T(8,128)S(1)}, u32[]{:S(2)}, u32[]{:S(2)}) collective-permute-start(f32[64,512]{1,0:T(8,128)S(1)} %get-tuple-element.32), channel_id=1, source_target_pairs={{0,1},{1,0},{2,3},{3,2},{4,5},{5,4},{6,7},{7,6},{8,9},{9,8},{10,11... | collective-permute-start | bytes 393224 | tf_op jit(solution)/shard_map/ppermute | solution.py:389
  22.7 8.9 %collective-permute-start.15 = (f32[64,512]{1,0:T(8,128)S(1)}, f32[64,512]{1,0:T(8,128)S(1)}, u32[]{:S(2)}, u32[]{:S(2)}) collective-permute-start(f32[64,512]{1,0:T(8,128)S(1)} %add.37), channel_id=1, source_target_pairs={{0,3},{1,2},{2,1},{3,0},{4,7},{5,6},{6,5},{7,4},{8,11},{9,10},{10,... | collective-permute-start | bytes 393224 | tf_op jit(solution)/shard_map/ppermute | solution.py:389
  25.9 6.3 %collective-permute-start.1 = (f32[16,768]{1,0:T(8,128)S(1)}, f32[16,768]{1,0:T(8,128)S(1)}, u32[]{:S(2)}, u32[]{:S(2)}) collective-permute-start(f32[16,768]{1,0:T(8,128)S(1)} %get-tuple-element.44), channel_id=1, source_target_pairs={{0,8},{4,12},{8,0},{12,4},{16,24},{20,28},{24,16},{28,20},{32,40},... | collective-permute-start | bytes 147464 | tf_op jit(solution)/shard_map/ppermute | solution.py:386
  26.0 7.7 %collective-permute-start.2 = (f32[16,768]{1,0:T(8,128)S(1)}, f32[16,768]{1,0:T(8,128)S(1)}, u32[]{:S(2)}, u32[]{:S(2)}) collective-permute-start(f32[16,768]{1,0:T(8,128)S(1)} %get-tuple-element.46), channel_id=1, source_target_pairs={{0,16},{4,20},{8,24},{12,28},{16,0},{20,4},{24,8},{28,12},{32,48},... | collective-permute-start | bytes 147464 | tf_op jit(solution)/shard_map/ppermute | solution.py:386
  31.1 4.1 %collective-permute-start.3 = (f32[16,768]{1,0:T(8,128)S(1)}, f32[16,768]{1,0:T(8,128)S(1)}, u32[]{:S(2)}, u32[]{:S(2)}) collective-permute-start(f32[16,768]{1,0:T(8,128)S(1)} %get-tuple-element.45), channel_id=1, source_target_pairs={{0,24},{4,28},{8,16},{12,20},{16,8},{20,12},{24,0},{28,4},{32,56},... | collective-permute-start | bytes 147464 | tf_op jit(solution)/shard_map/ppermute | solution.py:386
  31.7 13.1 %collective-permute-start.16 = (f32[64,512]{1,0:T(8,128)S(1)}, f32[64,512]{1,0:T(8,128)S(1)}, u32[]{:S(2)}, u32[]{:S(2)}) collective-permute-start(f32[64,512]{1,0:T(8,128)S(1)} %get-tuple-element.38.mine_up), channel_id=1, source_target_pairs={{0,3},{1,2},{2,1},{3,0},{4,7},{5,6},{6,5},{7,4},{8,11},{9,10},{10,... | collective-permute-start | bytes 393224 | tf_op jit(solution)/shard_map/ppermute | solution.py:389
  35.2 4.2 %collective-permute-start.4 = (f32[16,768]{1,0:T(8,128)S(1)}, f32[16,768]{1,0:T(8,128)S(1)}, u32[]{:S(2)}, u32[]{:S(2)}) collective-permute-start(f32[16,768]{1,0:T(8,128)S(1)} %fusion.1), channel_id=1, source_target_pairs={{0,32},{4,36},{8,40},{12,44},{16,48},{20,52},{24,56},{28,60},{32,0... | collective-permute-start | bytes 147464 | tf_op jit(solution)/shard_map/ppermute | solution.py:386
  39.4 8.5 %collective-permute-start.5 = (f32[16,768]{1,0:T(8,128)S(1)}, f32[16,768]{1,0:T(8,128)S(1)}, u32[]{:S(2)}, u32[]{:S(2)}) collective-permute-start(f32[16,768]{1,0:T(8,128)S(1)} %add.34), channel_id=1, source_target_pairs={{0,128},{4,132},{8,136},{12,140},{16,144},{20,148},{24,152},{28,15... | collective-permute-start | bytes 147464 | tf_op jit(solution)/shard_map/ppermute | solution.py:386
  44.5 10.2 %collective-permute-start.17 = (f32[64,512]{1,0:T(8,128)S(1)}, f32[64,512]{1,0:T(8,128)S(1)}, u32[]{:S(2)}, u32[]{:S(2)}) collective-permute-start(f32[64,512]{1,0:T(8,128)S(1)} %get-tuple-element.38.mine_up), channel_id=1, source_target_pairs={{0,1},{1,0},{2,3},{3,2},{4,5},{5,4},{6,7},{7,6},{8,9},{9,8},{10,11... | collective-permute-start | bytes 393224 | tf_op jit(solution)/shard_map/ppermute | solution.py:389
  44.8 9.9 %collective-permute-start.18 = (f32[64,512]{1,0:T(8,128)S(1)}, f32[64,512]{1,0:T(8,128)S(1)}, u32[]{:S(2)}, u32[]{:S(2)}) collective-permute-start(f32[64,512]{1,0:T(8,128)S(1)} %collective-permute-done.16.third_up), channel_id=1, source_target_pairs={{0,1},{1,0},{2,3},{3,2},{4,5},{5,4},{6,7},{7,6},{8,9},{9,8},{10,11... | collective-permute-start | bytes 393224 | tf_op jit(solution)/shard_map/ppermute | solution.py:389
  47.9 5.1 %collective-permute-start.6 = (f32[16,768]{1,0:T(8,128)S(1)}, f32[16,768]{1,0:T(8,128)S(1)}, u32[]{:S(2)}, u32[]{:S(2)}) collective-permute-start(f32[16,768]{1,0:T(8,128)S(1)} %add.35), channel_id=1, source_target_pairs={{0,64},{4,68},{8,72},{12,76},{16,80},{20,84},{24,88},{28,92},{32,9... | collective-permute-start | bytes 147464 | tf_op jit(solution)/shard_map/ppermute | solution.py:386
  53.0 9.9 %collective-permute-start.7 = (f32[16,768]{1,0:T(8,128)S(1)}, f32[16,768]{1,0:T(8,128)S(1)}, u32[]{:S(2)}, u32[]{:S(2)}) collective-permute-start(f32[16,768]{1,0:T(8,128)S(1)} %add.36), channel_id=1, source_target_pairs={{0,4},{4,0},{8,12},{12,8},{16,20},{20,16},{24,28},{28,24},{32,36},... | collective-permute-start | bytes 147464 | tf_op jit(solution)/shard_map/ppermute | solution.py:386
  61.1 16.7 %collective-permute-start.19 = (f32[64,512]{1,0:T(8,128)S(1)}, f32[64,512]{1,0:T(8,128)S(1)}, u32[]{:S(2)}, u32[]{:S(2)}) collective-permute-start(f32[64,512]{1,0:T(8,128)S(1)} %get-tuple-element.42), channel_id=1, source_target_pairs={{0,4},{4,8},{8,12},{12,16},{16,20},{20,24},{24,28},{28,32},{32,36}... | collective-permute-start | bytes 393224 | tf_op jit(solution)/shard_map/ppermute | solution.py:383
  61.2 16.6 %collective-permute-start.20 = (f32[64,512]{1,0:T(8,128)S(1)}, f32[64,512]{1,0:T(8,128)S(1)}, u32[]{:S(2)}, u32[]{:S(2)}) collective-permute-start(f32[64,512]{1,0:T(8,128)S(1)} %get-tuple-element.43), channel_id=1, source_target_pairs={{0,252},{4,0},{8,4},{12,8},{16,12},{20,16},{24,20},{28,24},{32,28}... | collective-permute-start | bytes 393224 | tf_op jit(solution)/shard_map/ppermute | solution.py:383
  62.9 7.5 %collective-permute-start.10 = (f32[32,768]{1,0:T(8,128)S(1)}, f32[32,768]{1,0:T(8,128)S(1)}, u32[]{:S(2)}, u32[]{:S(2)}) collective-permute-start(f32[32,768]{1,0:T(8,128)S(1)} %pad_maximum_fusion.mine), channel_id=1, source_target_pairs={{0,24},{4,28},{8,16},{12,20},{16,8},{20,12},{24,0},{28,4},{32,56},... | collective-permute-start | bytes 294920 | tf_op jit(solution)/shard_map/ppermute | solution.py:386
  63.0 10.0 %collective-permute-start.8 = (f32[32,768]{1,0:T(8,128)S(1)}, f32[32,768]{1,0:T(8,128)S(1)}, u32[]{:S(2)}, u32[]{:S(2)}) collective-permute-start(f32[32,768]{1,0:T(8,128)S(1)} %pad_maximum_fusion.mine), channel_id=1, source_target_pairs={{0,8},{4,12},{8,0},{12,4},{16,24},{20,28},{24,16},{28,20},{32,40},... | collective-permute-start | bytes 294920 | tf_op jit(solution)/shard_map/ppermute | solution.py:386
  70.4 6.1 %collective-permute-start.9 = (f32[32,768]{1,0:T(8,128)S(1)}, f32[32,768]{1,0:T(8,128)S(1)}, u32[]{:S(2)}, u32[]{:S(2)}) collective-permute-start(f32[32,768]{1,0:T(8,128)S(1)} %pad_maximum_fusion.mine), channel_id=1, source_target_pairs={{0,16},{4,20},{8,24},{12,28},{16,0},{20,4},{24,8},{28,12},{32,48},... | collective-permute-start | bytes 294920 | tf_op jit(solution)/shard_map/ppermute | solution.py:386

commit v3 on v2

--- a/solution.py
+++ b/solution.py
@@ -77,11 +77,12 @@
     return (lane < bound).astype(f32)
 
 
-def pack_kernel(counts, features, positions, packed):
+def pack_kernel(counts, features, positions, cotangent, packed, cot_masked):
     live = live_row(counts)
     packed[0:ROWS, :] = features[...] * live
     packed[ROWS : ROWS + 3, :] = positions[...]
     packed[ROWS + 3 : PACK, :] = jnp.broadcast_to(live, (PACK - ROWS - 3, LAYER))
+    cot_masked[...] = cotangent[...] * live
 
 
 def forward_filter_kernel(filters, forward):
@@ -92,7 +93,7 @@
     forward[:, 1024:1536] = high
 
 
-def backward_filter_kernel(filters, wavevectors, screened, backward, weights):
+def backward_filter_kernel(filters, wavevectors, screened, own, below, above, backward, weights, columns, lines):
     for r in range(NRAD):
         rows = slice(ROWS * r, ROWS * r + ROWS)
         high, low = split(filters[r] * TERM[r])
@@ -115,6 +116,16 @@
     norm = jnp.sum(value * screened[0:1, :], 1, keepdims=True)
     value = value * (FACTOR / jnp.sqrt(norm))
     weights[...] = jnp.concatenate([value, value], 1)
+    flipped = own[ROWS:PACK, :].T * SCALE
+    for a in range(3):
+        columns[a] = jnp.broadcast_to(flipped[:, a : a + 1], (LAYER, 128))
+    for section, source in enumerate((below, own, above)):
+        for side in range(4):
+            for a in range(3):
+                at = slice(ROWS + a, ROWS + a + 1)
+                shift = (section - 1.0) * SCALE if a == 0 else 0.0
+                lines[4 * section + side, a : a + 1, :] = source[at, 128 * side : 128 * side + 128] * SCALE + shift
+    lines[12] = jnp.full((8, 128), 1e4, f32)
 
 
 def trig(turns):
@@ -125,7 +136,7 @@
     return 1 - 2 * s * s, 2 * s * c
 
 
-def structure_kernel(packed, cotangent, digits, keep, send, cot_masked, table_high, table_low, sums):
+def structure_kernel(packed, cot_masked, digits, keep, send, table_high, table_low, sums):
     space = lax.axis_index("space")
     core, x = space % 2, (space // 2) % 4
     row_x = (packed[ROWS : ROWS + 1, :] + space.astype(f32)) * (1 / 64)
@@ -149,9 +160,7 @@
         put(160 + 40 * n, cc - ss, sc + cs)
         put(160 - 40 * n, cc + ss, sc - cs)
     masked_high, masked_low = split(packed[0:ROWS, :])
-    cot = cotangent[...] * packed[ROWS + 3 : ROWS + 4, :]
-    cot_masked[...] = cot
-    cot_high, cot_low = split(cot)
+    cot_high, cot_low = split(cot_masked[...])
     fields = jnp.concatenate([masked_high, cot_high, masked_low, cot_low], 0)
     both = dot(fields, table_high[...], NT) + dot(fields, table_low[...], NT)
     sums[...] = both[:128] + both[128:]
@@ -284,8 +293,8 @@
     upstream[...] = cot_masked[...] * (sigma * (1.0 + pre * (1.0 - sigma)))
 
 
-def backward_kernel(neighbours, own, below, above, filters, mine_up, third_up, near_up, far_up,
-                    low_side, middle, high_side, columns, lines, amounts, pieces, panels, cots, left, right, sums):
+def backward_kernel(neighbours, own, below, above, filters, columns, lines, mine_up, third_up, near_up, far_up,
+                    low_side, middle, high_side, amounts, pieces, panels, cots, left, right, sums):
     mine = lax.axis_index("chan")
     sources = (below, own, above)
     count_live(sources, amounts)
@@ -296,16 +305,6 @@
         panels[pl.ds(pl.multiple_of(at, ROWS), ROWS), :] = first
         panels[pl.ds(pl.multiple_of(at + 256, ROWS), ROWS), :] = second
         panels[pl.ds(pl.multiple_of(at + 512, ROWS), ROWS), :] = first
-    flipped = own[ROWS:PACK, :].T * SCALE
-    for a in range(3):
-        columns[a] = jnp.broadcast_to(flipped[:, a : a + 1], (LAYER, 128))
-    for section, source in enumerate(sources):
-        for side in range(4):
-            for a in range(3):
-                at = slice(ROWS + a, ROWS + a + 1)
-                shift = (section - 1.0) * SCALE if a == 0 else 0.0
-                lines[4 * section + side, a : a + 1, :] = source[at, 128 * side : 128 * side + 128] * SCALE + shift
-    lines[12] = jnp.full((8, 128), 1e4, f32)
     cot = dot(filters[...], panels[...])
     for r in range(NRAD):
         first, second = split(cot[ROWS * r : ROWS * r + ROWS])
@@ -388,18 +387,20 @@
     def chan_swap(v, mask):
         return lax.ppermute(v, "chan", [(i, i ^ mask) for i in range(4)])
 
-    packed = call(pack_kernel, shape(PACK, LAYER), 1, 2, far=(1, 2))(counts, features, positions)
+    packed, cot_masked = call(
+        pack_kernel, (shape(PACK, LAYER), shape(ROWS, LAYER)), 1, 3, far=(1, 2, 3)
+    )(counts, features, positions, cotangent)
     below = shift(packed, 1)
     above = shift(packed, -1)
 
     digits = np.zeros((HALF, 8), np.float32)
     digits[:, :3] = np.stack(half_space(), 1)
-    keep, send, cot_masked, table_high, table_low = call(
+    keep, send, table_high, table_low = call(
         structure_kernel,
-        (shape(ROWS, 768), shape(ROWS, 768), shape(ROWS, LAYER),
+        (shape(ROWS, 768), shape(ROWS, 768),
          shape(768, LAYER, dtype=bf16), shape(768, LAYER, dtype=bf16)),
-        0, 3, [pltpu.VMEM((128, 768), f32)], far=(1, 2),
-    )(packed, cotangent, jnp.asarray(digits))
+        0, 3, [pltpu.VMEM((128, 768), f32)], far=(2,),
+    )(packed, cot_masked, jnp.asarray(digits[:40]))
     forward_filters = call(forward_filter_kernel, shape(256, 1536, dtype=bf16), 0, 1, far=(0,))(filters)
     half = keep + swap(send, 1)
     got = []
@@ -431,10 +432,11 @@
     third_panel = third_panel + far
     third = chan_swap(third_panel, 3)
     quarter = quarter + swap(quarter, 16)
-    backward_filters, weights = call(
-        backward_filter_kernel, (shape(512, 768, dtype=bf16), shape(1, 768)), 0, 3,
-        far=(0, 1, 2),
-    )(filters, wavevectors, jnp.asarray(screening()))
+    backward_filters, weights, columns, lines = call(
+        backward_filter_kernel,
+        (shape(512, 768, dtype=bf16), shape(1, 768), shape(3, LAYER, 128), shape(13, 8, 128)),
+        0, 6, far=(0, 1, 2),
+    )(filters, wavevectors, jnp.asarray(screening()), packed, below, above)
     activated, upstream = call(
         activation_kernel, (shape(ROWS, LAYER), shape(ROWS, LAYER)), 0, 4
     )(own_panel, near, third, cot_masked)
@@ -446,10 +448,8 @@
     for d in (1, 2, 3):
         got.append(swap(pair, 2 * d))
     left, middle, right = call(
-        backward_kernel, tuple([shape(ROWS, LAYER)] * 3), 1, 8,
+        backward_kernel, tuple([shape(ROWS, LAYER)] * 3), 1, 10,
         [
-            pltpu.VMEM((3, LAYER, 128), f32),
-            pltpu.VMEM((13, 8, 128), f32),
             pltpu.SMEM((6,), jnp.int32),
             pltpu.SMEM((10,), jnp.int32),
             pltpu.VMEM((768, LAYER), bf16),
@@ -458,7 +458,8 @@
             pltpu.VMEM((2048, 128), bf16),
             pltpu.VMEM((13 * 128, 128), f32),
         ],
-    )(neighbours, packed, below, above, backward_filters, upstream, third_up, near_up, far_up)
+    )(neighbours, packed, below, above, backward_filters, columns, lines,
+      upstream, third_up, near_up, far_up)
     from_lower = shift(right, 1)
     from_upper = shift(left, -1)
     updated, partial = call(

time: 78.8 us -> 78.8 us (level)
    ppermute x11, starting transfers between devices: 18.9 us -> 18 us  [swap(): return lax.ppermute(v, 'space', [(i, i ^ mask) for i in range(n_space)])]
  transfers between devices with their start and end apart: 21 -> 21, of which waited for: 8 -> 8; matrix products, arithmetic and copies ran while one was open for 0% -> 0% of each run, Pallas kernels for 29% -> 28%
where the time goes in v3:
time: 78.8 us; the launch traced here: 78.5 us
  starting transfers between devices  29.9 us (38%)
  waiting for transfers between devices  23.7 us (30%)
  Pallas kernels  23.3 us (30%)
  between operations  0.81 us (1%)
    pallas_call x9, Pallas kernels, place(): run(*[put(v, pltpu.HBM if k < n_smem or k in far else pltpu.VMEM) for k,...  23.3 us
    ppermute x11, waiting for transfers between devices, swap(): return lax.ppermute(v, 'space', [(i, i ^ mask) for i in range(n_space)])  19.5 us
    ppermute x11, starting transfers between devices, swap(): return lax.ppermute(v, 'space', [(i, i ^ mask) for i in range(n_space)])  18 us
    ppermute x6, starting transfers between devices, chan_swap(): return lax.ppermute(v, 'chan', [(i, i ^ mask) for i in range(4)])  8.2 us
    ppermute x6, waiting for transfers between devices, chan_swap(): return lax.ppermute(v, 'chan', [(i, i ^ mask) for i in range(4)])  4.23 us
    ppermute x4, starting transfers between devices, shift(): lax.ppermute(v, 'space', [(i, (i + d) % n_space) for i in range(n_space)])  3.63 us
  transfers between devices with their start and end apart: 21, of which 8 were waited for; matrix products, arithmetic and copies ran while one was open for 0% of the time, Pallas kernels for 28%

profile of v3, /device:TPU:4, one launch (start us, length us, event | category | flops | bytes accessed | tf_op | source)
XLA Modules:
  0.0 78.5 jit_solution(2856784423549473164)
XLA Ops:
  0.6 1.0 %shard_map.104 = (f32[72,512]{1,0:T(8,128)S(1)}, f32[64,512]{1,0:T(8,128)S(1)}) custom-call(s32[2]{0:T(128)} %counts.1, f32[64,512]{1,0:T(8,128)} %features.1, f32[3,512]{1,0:T(4,128)} %positions.1, f32[64,512]{1,0:T(8,128)} %cotangent.1), custom_call_target="tpu_custom_call" | custom-call | tf_op jit(solution)/shard_map/pallas_call | solution.py:67
  1.7 1.7 %collective-permute-start.12 = (f32[72,512]{1,0:T(8,128)S(1)}, f32[72,512]{1,0:T(8,128)S(1)}, u32[]{:S(2)}, u32[]{:S(2)}) collective-permute-start(f32[72,512]{1,0:T(8,128)S(1)} %get-tuple-element.26.packed.own), channel_id=1, source_target_pairs={{0,252},{4,0},{8,4},{12,8},{16,12},{20,16},{24,20},{28,24},{32,28}... | collective-permute-start | bytes 442376 | tf_op jit(solution)/shard_map/ppermute | solution.py:382
  3.5 1.7 %shard_map.105 = (f32[64,768]{1,0:T(8,128)S(1)}, f32[64,768]{1,0:T(8,128)S(1)}, bf16[768,512]{1,0:T(8,128)(2,1)S(1)}, bf16[768,512]{1,0:T(8,128)(2,1)S(1)}) custom-call(f32[72,512]{1,0:T(8,128)S(1)} %get-tuple-element.26.packed.own, f32[64,512]{1,0:T(8,128)S(1)} %get-tuple-element.27.cot_masked, f32[40,8]{1,0:T(8,128)} %constant.4.clone.digits), custom_call_target="tpu_custom_call" | custom-call | tf_op jit(solution)/shard_map/pallas_call | solution.py:67
  5.3 1.3 %shard_map.107.filters = bf16[256,1536]{1,0:T(8,128)(2,1)S(1)} custom-call(f32[8,64,256]{2,1,0:T(8,128)} %filters.3), custom_call_target="tpu_custom_call" | custom-call | tf_op jit(solution)/shard_map/pallas_call | solution.py:67
  6.6 5.3 %shard_map.108 = (f32[256,256]{1,0:T(8,128)S(1)}, f32[1664,8]{1,0:T(8,128)S(1)}, bf16[12,128,128]{2,1,0:T(8,128)(2,1)S(1)}) custom-call(s32[2,4]{1,0:T(2,128)} %neighbours.5, f32[72,512]{1,0:T(8,128)S(1)} %get-tuple-element.26.packed.own, f32[72,512]{1,0:T(8,128)S(1)} %collective-permute-done.11.below, f32[72,512]{1,0:T(8,128)S(1)} %collective-permute-done.12.above, ...), custom_call_target="tpu_custom_call" | custom-call | tf_op jit(solution)/shard_map/pallas_call | solution.py:67
  11.9 4.6 %shard_map.109 = (f32[64,512]{1,0:T(8,128)S(1)}, f32[64,512]{1,0:T(8,128)S(1)}, f32[64,512]{1,0:T(8,128)S(1)}, f32[64,512]{1,0:T(8,128)S(1)}) custom-call(s32[2,4]{1,0:T(2,128)} %neighbours.5, f32[72,512]{1,0:T(8,128)S(1)} %get-tuple-element.26.packed.own, f32[72,512]{1,0:T(8,128)S(1)} %collective-permute-done.11.below, ...), custom_call_target="tpu_custom_call" | custom-call | tf_op jit(solution)/shard_map/pallas_call | solution.py:67
  16.5 1.7 %collective-permute-start.14 = (f32[64,512]{1,0:T(8,128)S(1)}, f32[64,512]{1,0:T(8,128)S(1)}, u32[]{:S(2)}, u32[]{:S(2)}) collective-permute-start(f32[64,512]{1,0:T(8,128)S(1)} %get-tuple-element.39), channel_id=1, source_target_pairs={{0,1},{1,0},{2,3},{3,2},{4,5},{5,4},{6,7},{7,6},{8,9},{9,8},{10,11... | collective-permute-start | bytes 393224 | tf_op jit(solution)/shard_map/ppermute | solution.py:388
  18.6 4.2 %collective-permute-done.14 = f32[64,512]{1,0:T(8,128)S(1)} collective-permute-done((f32[64,512]{1,0:T(8,128)S(1)}, f32[64,512]{1,0:T(8,128)S(1)}, u32[]{:S(2)}, u32[]{:S(2)}) %collective-permute-start.14) | collective-permute-done | bytes 131104 | tf_op jit(solution)/shard_map/ppermute | solution.py:388
  22.8 3.1 %collective-permute-start.15 = (f32[64,512]{1,0:T(8,128)S(1)}, f32[64,512]{1,0:T(8,128)S(1)}, u32[]{:S(2)}, u32[]{:S(2)}) collective-permute-start(f32[64,512]{1,0:T(8,128)S(1)} %add.37), channel_id=1, source_target_pairs={{0,3},{1,2},{2,1},{3,0},{4,7},{5,6},{6,5},{7,4},{8,11},{9,10},{10,... | collective-permute-start | bytes 393224 | tf_op jit(solution)/shard_map/ppermute | solution.py:388
  26.1 4.9 %collective-permute-start.2 = (f32[16,768]{1,0:T(8,128)S(1)}, f32[16,768]{1,0:T(8,128)S(1)}, u32[]{:S(2)}, u32[]{:S(2)}) collective-permute-start(f32[16,768]{1,0:T(8,128)S(1)} %get-tuple-element.52), channel_id=1, source_target_pairs={{0,16},{4,20},{8,24},{12,28},{16,0},{20,4},{24,8},{28,12},{32,48},... | collective-permute-start | bytes 147464 | tf_op jit(solution)/shard_map/ppermute | solution.py:385
  32.5 1.0 %collective-permute-done.2 = f32[16,768]{1,0:T(8,128)S(1)} collective-permute-done((f32[16,768]{1,0:T(8,128)S(1)}, f32[16,768]{1,0:T(8,128)S(1)}, u32[]{:S(2)}, u32[]{:S(2)}) %collective-permute-start.2) | collective-permute-done | bytes 49184 | tf_op jit(solution)/shard_map/ppermute | solution.py:385
  33.4 1.6 %collective-permute-done.3 = f32[16,768]{1,0:T(8,128)S(1)} collective-permute-done((f32[16,768]{1,0:T(8,128)S(1)}, f32[16,768]{1,0:T(8,128)S(1)}, u32[]{:S(2)}, u32[]{:S(2)}) %collective-permute-start.3) | collective-permute-done | bytes 49184 | tf_op jit(solution)/shard_map/ppermute | solution.py:385
  35.2 4.1 %collective-permute-done.4 = f32[16,768]{1,0:T(8,128)S(1)} collective-permute-done((f32[16,768]{1,0:T(8,128)S(1)}, f32[16,768]{1,0:T(8,128)S(1)}, u32[]{:S(2)}, u32[]{:S(2)}) %collective-permute-start.4) | collective-permute-done | bytes 49184 | tf_op jit(solution)/shard_map/ppermute | solution.py:385
  39.2 4.8 %collective-permute-start.5 = (f32[16,768]{1,0:T(8,128)S(1)}, f32[16,768]{1,0:T(8,128)S(1)}, u32[]{:S(2)}, u32[]{:S(2)}) collective-permute-start(f32[16,768]{1,0:T(8,128)S(1)} %add.34), channel_id=1, source_target_pairs={{0,128},{4,132},{8,136},{12,140},{16,144},{20,148},{24,152},{28,15... | collective-permute-start | bytes 147464 | tf_op jit(solution)/shard_map/ppermute | solution.py:385
  44.3 1.8 %collective-permute-start.18 = (f32[64,512]{1,0:T(8,128)S(1)}, f32[64,512]{1,0:T(8,128)S(1)}, u32[]{:S(2)}, u32[]{:S(2)}) collective-permute-start(f32[64,512]{1,0:T(8,128)S(1)} %collective-permute-done.16.third_up), channel_id=1, source_target_pairs={{0,1},{1,0},{2,3},{3,2},{4,5},{5,4},{6,7},{7,6},{8,9},{9,8},{10,11... | collective-permute-start | bytes 393224 | tf_op jit(solution)/shard_map/ppermute | solution.py:388
  46.1 1.7 %collective-permute-done.5 = f32[16,768]{1,0:T(8,128)S(1)} collective-permute-done((f32[16,768]{1,0:T(8,128)S(1)}, f32[16,768]{1,0:T(8,128)S(1)}, u32[]{:S(2)}, u32[]{:S(2)}) %collective-permute-start.5) | collective-permute-done | bytes 49184 | tf_op jit(solution)/shard_map/ppermute | solution.py:385
  47.9 5.0 %collective-permute-done.6 = f32[16,768]{1,0:T(8,128)S(1)} collective-permute-done((f32[16,768]{1,0:T(8,128)S(1)}, f32[16,768]{1,0:T(8,128)S(1)}, u32[]{:S(2)}, u32[]{:S(2)}) %collective-permute-start.6) | collective-permute-done | bytes 49184 | tf_op jit(solution)/shard_map/ppermute | solution.py:385
  53.0 1.8 %shard_map.106 = (bf16[512,768]{1,0:T(8,128)(2,1)S(1)}, f32[1,768]{1,0:T(1,128)S(1)}, f32[3,512,128]{2,1,0:T(8,128)S(1)}, f32[13,8,128]{2,1,0:T(8,128)S(1)}) custom-call(f32[8,64,256]{2,1,0:T(8,128)} %filters.3, s32[3,512]{1,0:T(4,128)} %wavevectors.1, f32[8,384]{1,0:T(8,128)} %constant.5.clone.screened, f32[72,512]{1,0:T(8,128)S(1)} %get-tuple-element.26.packed.own, ...), custom_call_target="tpu_custom_call" | custom-call | tf_op jit(solution)/shard_map/pallas_call | solution.py:67
  54.8 6.3 %shard_map.111 = (f32[64,512]{1,0:T(8,128)S(1)}, f32[64,512]{1,0:T(8,128)S(1)}, f32[64,512]{1,0:T(8,128)S(1)}) custom-call(s32[2,4]{1,0:T(2,128)} %neighbours.5, f32[72,512]{1,0:T(8,128)S(1)} %get-tuple-element.26.packed.own, f32[72,512]{1,0:T(8,128)S(1)} %collective-permute-done.11.below, f32[72,512]{1,0:T(8,128)S(1)} %collective-permute-done.12.above, ...), custom_call_target="tpu_custom_call" | custom-call | tf_op jit(solution)/shard_map/pallas_call | solution.py:67
  61.2 1.7 %collective-permute-start.20 = (f32[64,512]{1,0:T(8,128)S(1)}, f32[64,512]{1,0:T(8,128)S(1)}, u32[]{:S(2)}, u32[]{:S(2)}) collective-permute-start(f32[64,512]{1,0:T(8,128)S(1)} %get-tuple-element.49), channel_id=1, source_target_pairs={{0,252},{4,0},{8,4},{12,8},{16,12},{20,16},{24,20},{28,24},{32,28}... | collective-permute-start | bytes 393224 | tf_op jit(solution)/shard_map/ppermute | solution.py:382
  63.1 7.3 %collective-permute-start.8 = (f32[32,768]{1,0:T(8,128)S(1)}, f32[32,768]{1,0:T(8,128)S(1)}, u32[]{:S(2)}, u32[]{:S(2)}) collective-permute-start(f32[32,768]{1,0:T(8,128)S(1)} %pad_maximum_fusion.mine), channel_id=1, source_target_pairs={{0,8},{4,12},{8,0},{12,4},{16,24},{20,28},{24,16},{28,20},{32,40},... | collective-permute-start | bytes 294920 | tf_op jit(solution)/shard_map/ppermute | solution.py:385
  70.4 2.6 %collective-permute-done.8.one = f32[32,768]{1,0:T(8,128)S(1)} collective-permute-done((f32[32,768]{1,0:T(8,128)S(1)}, f32[32,768]{1,0:T(8,128)S(1)}, u32[]{:S(2)}, u32[]{:S(2)}) %collective-permute-start.8) | collective-permute-done | bytes 98336 | tf_op jit(solution)/shard_map/ppermute | solution.py:385
  73.0 3.5 %collective-permute-done.9.two = f32[32,768]{1,0:T(8,128)S(1)} collective-permute-done((f32[32,768]{1,0:T(8,128)S(1)}, f32[32,768]{1,0:T(8,128)S(1)}, u32[]{:S(2)}, u32[]{:S(2)}) %collective-permute-start.9) | collective-permute-done | bytes 98336 | tf_op jit(solution)/shard_map/ppermute | solution.py:385
  76.5 1.3 %shard_map.112 = (f32[64,512]{1,0:T(8,128)}, f32[64,512]{1,0:T(8,128)S(1)}) custom-call(f32[32,768]{1,0:T(8,128)S(1)} %pad_maximum_fusion.mine, f32[32,768]{1,0:T(8,128)S(1)} %collective-permute-done.8.one, f32[32,768]{1,0:T(8,128)S(1)} %collective-permute-done.9.two, f32[32,768]{1,0:T(8,128)S(1)} %collective-permute-done.10.three, ...), custom_call_target="tpu_custom_call" | custom-call | tf_op jit(solution)/shard_map/pallas_call | solution.py:67
  (37 shorter events, 3.7 us)
Async XLA Ops:
  1.7 4.9 %collective-permute-start.11 = (f32[72,512]{1,0:T(8,128)S(1)}, f32[72,512]{1,0:T(8,128)S(1)}, u32[]{:S(2)}, u32[]{:S(2)}) collective-permute-start(f32[72,512]{1,0:T(8,128)S(1)} %get-tuple-element.26.packed.own), channel_id=1, source_target_pairs={{0,4},{4,8},{8,12},{12,16},{16,20},{20,24},{24,28},{28,32},{32,36}... | collective-permute-start | bytes 442376 | tf_op jit(solution)/shard_map/ppermute | solution.py:382
  1.7 4.9 %collective-permute-start.12 = (f32[72,512]{1,0:T(8,128)S(1)}, f32[72,512]{1,0:T(8,128)S(1)}, u32[]{:S(2)}, u32[]{:S(2)}) collective-permute-start(f32[72,512]{1,0:T(8,128)S(1)} %get-tuple-element.26.packed.own), channel_id=1, source_target_pairs={{0,252},{4,0},{8,4},{12,8},{16,12},{20,16},{24,20},{28,24},{32,28}... | collective-permute-start | bytes 442376 | tf_op jit(solution)/shard_map/ppermute | solution.py:382
  5.2 13.3 %collective-permute-start = (f32[64,768]{1,0:T(8,128)S(1)}, f32[64,768]{1,0:T(8,128)S(1)}, u32[]{:S(2)}, u32[]{:S(2)}) collective-permute-start(f32[64,768]{1,0:T(8,128)S(1)} %get-tuple-element.29), channel_id=1, source_target_pairs={{0,4},{4,0},{8,12},{12,8},{16,20},{20,16},{24,28},{28,24},{32,36},... | collective-permute-start | bytes 589832 | tf_op jit(solution)/shard_map/ppermute | solution.py:385
  16.5 6.4 %collective-permute-start.14 = (f32[64,512]{1,0:T(8,128)S(1)}, f32[64,512]{1,0:T(8,128)S(1)}, u32[]{:S(2)}, u32[]{:S(2)}) collective-permute-start(f32[64,512]{1,0:T(8,128)S(1)} %get-tuple-element.39), channel_id=1, source_target_pairs={{0,1},{1,0},{2,3},{3,2},{4,5},{5,4},{6,7},{7,6},{8,9},{9,8},{10,11... | collective-permute-start | bytes 393224 | tf_op jit(solution)/shard_map/ppermute | solution.py:388
  18.1 13.3 %collective-permute-start.13 = (f32[64,512]{1,0:T(8,128)S(1)}, f32[64,512]{1,0:T(8,128)S(1)}, u32[]{:S(2)}, u32[]{:S(2)}) collective-permute-start(f32[64,512]{1,0:T(8,128)S(1)} %get-tuple-element.37), channel_id=1, source_target_pairs={{0,1},{1,0},{2,3},{3,2},{4,5},{5,4},{6,7},{7,6},{8,9},{9,8},{10,11... | collective-permute-start | bytes 393224 | tf_op jit(solution)/shard_map/ppermute | solution.py:388
  22.8 8.6 %collective-permute-start.15 = (f32[64,512]{1,0:T(8,128)S(1)}, f32[64,512]{1,0:T(8,128)S(1)}, u32[]{:S(2)}, u32[]{:S(2)}) collective-permute-start(f32[64,512]{1,0:T(8,128)S(1)} %add.37), channel_id=1, source_target_pairs={{0,3},{1,2},{2,1},{3,0},{4,7},{5,6},{6,5},{7,4},{8,11},{9,10},{10,... | collective-permute-start | bytes 393224 | tf_op jit(solution)/shard_map/ppermute | solution.py:388
  26.0 6.5 %collective-permute-start.1 = (f32[16,768]{1,0:T(8,128)S(1)}, f32[16,768]{1,0:T(8,128)S(1)}, u32[]{:S(2)}, u32[]{:S(2)}) collective-permute-start(f32[16,768]{1,0:T(8,128)S(1)} %get-tuple-element.50), channel_id=1, source_target_pairs={{0,8},{4,12},{8,0},{12,4},{16,24},{20,28},{24,16},{28,20},{32,40},... | collective-permute-start | bytes 147464 | tf_op jit(solution)/shard_map/ppermute | solution.py:385
  26.1 7.4 %collective-permute-start.2 = (f32[16,768]{1,0:T(8,128)S(1)}, f32[16,768]{1,0:T(8,128)S(1)}, u32[]{:S(2)}, u32[]{:S(2)}) collective-permute-start(f32[16,768]{1,0:T(8,128)S(1)} %get-tuple-element.52), channel_id=1, source_target_pairs={{0,16},{4,20},{8,24},{12,28},{16,0},{20,4},{24,8},{28,12},{32,48},... | collective-permute-start | bytes 147464 | tf_op jit(solution)/shard_map/ppermute | solution.py:385
  30.9 4.1 %collective-permute-start.3 = (f32[16,768]{1,0:T(8,128)S(1)}, f32[16,768]{1,0:T(8,128)S(1)}, u32[]{:S(2)}, u32[]{:S(2)}) collective-permute-start(f32[16,768]{1,0:T(8,128)S(1)} %get-tuple-element.51), channel_id=1, source_target_pairs={{0,24},{4,28},{8,16},{12,20},{16,8},{20,12},{24,0},{28,4},{32,56},... | collective-permute-start | bytes 147464 | tf_op jit(solution)/shard_map/ppermute | solution.py:385
  31.5 12.8 %collective-permute-start.16 = (f32[64,512]{1,0:T(8,128)S(1)}, f32[64,512]{1,0:T(8,128)S(1)}, u32[]{:S(2)}, u32[]{:S(2)}) collective-permute-start(f32[64,512]{1,0:T(8,128)S(1)} %get-tuple-element.44.mine_up), channel_id=1, source_target_pairs={{0,3},{1,2},{2,1},{3,0},{4,7},{5,6},{6,5},{7,4},{8,11},{9,10},{10,... | collective-permute-start | bytes 393224 | tf_op jit(solution)/shard_map/ppermute | solution.py:388
  35.1 4.2 %collective-permute-start.4 = (f32[16,768]{1,0:T(8,128)S(1)}, f32[16,768]{1,0:T(8,128)S(1)}, u32[]{:S(2)}, u32[]{:S(2)}) collective-permute-start(f32[16,768]{1,0:T(8,128)S(1)} %fusion.1), channel_id=1, source_target_pairs={{0,32},{4,36},{8,40},{12,44},{16,48},{20,52},{24,56},{28,60},{32,0... | collective-permute-start | bytes 147464 | tf_op jit(solution)/shard_map/ppermute | solution.py:385
  39.2 8.6 %collective-permute-start.5 = (f32[16,768]{1,0:T(8,128)S(1)}, f32[16,768]{1,0:T(8,128)S(1)}, u32[]{:S(2)}, u32[]{:S(2)}) collective-permute-start(f32[16,768]{1,0:T(8,128)S(1)} %add.34), channel_id=1, source_target_pairs={{0,128},{4,132},{8,136},{12,140},{16,144},{20,148},{24,152},{28,15... | collective-permute-start | bytes 147464 | tf_op jit(solution)/shard_map/ppermute | solution.py:385
  44.1 10.7 %collective-permute-start.17 = (f32[64,512]{1,0:T(8,128)S(1)}, f32[64,512]{1,0:T(8,128)S(1)}, u32[]{:S(2)}, u32[]{:S(2)}) collective-permute-start(f32[64,512]{1,0:T(8,128)S(1)} %get-tuple-element.44.mine_up), channel_id=1, source_target_pairs={{0,1},{1,0},{2,3},{3,2},{4,5},{5,4},{6,7},{7,6},{8,9},{9,8},{10,11... | collective-permute-start | bytes 393224 | tf_op jit(solution)/shard_map/ppermute | solution.py:388
  44.3 10.6 %collective-permute-start.18 = (f32[64,512]{1,0:T(8,128)S(1)}, f32[64,512]{1,0:T(8,128)S(1)}, u32[]{:S(2)}, u32[]{:S(2)}) collective-permute-start(f32[64,512]{1,0:T(8,128)S(1)} %collective-permute-done.16.third_up), channel_id=1, source_target_pairs={{0,1},{1,0},{2,3},{3,2},{4,5},{5,4},{6,7},{7,6},{8,9},{9,8},{10,11... | collective-permute-start | bytes 393224 | tf_op jit(solution)/shard_map/ppermute | solution.py:388
  47.8 5.1 %collective-permute-start.6 = (f32[16,768]{1,0:T(8,128)S(1)}, f32[16,768]{1,0:T(8,128)S(1)}, u32[]{:S(2)}, u32[]{:S(2)}) collective-permute-start(f32[16,768]{1,0:T(8,128)S(1)} %add.35), channel_id=1, source_target_pairs={{0,64},{4,68},{8,72},{12,76},{16,80},{20,84},{24,88},{28,92},{32,9... | collective-permute-start | bytes 147464 | tf_op jit(solution)/shard_map/ppermute | solution.py:385
  52.9 10.0 %collective-permute-start.7 = (f32[16,768]{1,0:T(8,128)S(1)}, f32[16,768]{1,0:T(8,128)S(1)}, u32[]{:S(2)}, u32[]{:S(2)}) collective-permute-start(f32[16,768]{1,0:T(8,128)S(1)} %add.36), channel_id=1, source_target_pairs={{0,4},{4,0},{8,12},{12,8},{16,20},{20,16},{24,28},{28,24},{32,36},... | collective-permute-start | bytes 147464 | tf_op jit(solution)/shard_map/ppermute | solution.py:385
  61.1 16.6 %collective-permute-start.19 = (f32[64,512]{1,0:T(8,128)S(1)}, f32[64,512]{1,0:T(8,128)S(1)}, u32[]{:S(2)}, u32[]{:S(2)}) collective-permute-start(f32[64,512]{1,0:T(8,128)S(1)} %get-tuple-element.48), channel_id=1, source_target_pairs={{0,4},{4,8},{8,12},{12,16},{16,20},{20,24},{24,28},{28,32},{32,36}... | collective-permute-start | bytes 393224 | tf_op jit(solution)/shard_map/ppermute | solution.py:382
  61.2 16.5 %collective-permute-start.20 = (f32[64,512]{1,0:T(8,128)S(1)}, f32[64,512]{1,0:T(8,128)S(1)}, u32[]{:S(2)}, u32[]{:S(2)}) collective-permute-start(f32[64,512]{1,0:T(8,128)S(1)} %get-tuple-element.49), channel_id=1, source_target_pairs={{0,252},{4,0},{8,4},{12,8},{16,12},{20,16},{24,20},{28,24},{32,28}... | collective-permute-start | bytes 393224 | tf_op jit(solution)/shard_map/ppermute | solution.py:382
  63.0 7.4 %collective-permute-start.10 = (f32[32,768]{1,0:T(8,128)S(1)}, f32[32,768]{1,0:T(8,128)S(1)}, u32[]{:S(2)}, u32[]{:S(2)}) collective-permute-start(f32[32,768]{1,0:T(8,128)S(1)} %pad_maximum_fusion.mine), channel_id=1, source_target_pairs={{0,24},{4,28},{8,16},{12,20},{16,8},{20,12},{24,0},{28,4},{32,56},... | collective-permute-start | bytes 294920 | tf_op jit(solution)/shard_map/ppermute | solution.py:385
  63.1 9.9 %collective-permute-start.8 = (f32[32,768]{1,0:T(8,128)S(1)}, f32[32,768]{1,0:T(8,128)S(1)}, u32[]{:S(2)}, u32[]{:S(2)}) collective-permute-start(f32[32,768]{1,0:T(8,128)S(1)} %pad_maximum_fusion.mine), channel_id=1, source_target_pairs={{0,8},{4,12},{8,0},{12,4},{16,24},{20,28},{24,16},{28,20},{32,40},... | collective-permute-start | bytes 294920 | tf_op jit(solution)/shard_map/ppermute | solution.py:385
  70.4 6.1 %collective-permute-start.9 = (f32[32,768]{1,0:T(8,128)S(1)}, f32[32,768]{1,0:T(8,128)S(1)}, u32[]{:S(2)}, u32[]{:S(2)}) collective-permute-start(f32[32,768]{1,0:T(8,128)S(1)} %pad_maximum_fusion.mine), channel_id=1, source_target_pairs={{0,16},{4,20},{8,24},{12,28},{16,0},{20,4},{24,8},{28,12},{32,48},... | collective-permute-start | bytes 294920 | tf_op jit(solution)/shard_map/ppermute | solution.py:385
